TPU v7x, 512 devices: a whole 4x4x16 slice. The times are simulated.
512 devices in a mesh: rows: 128 (over y, z, core), cols: 4 (over x).
Axes of the slice: x: 4, y: 4, z: 16, core: 2. Of those that a mesh axis runs over, the one named last changes fastest.
Arguments:
- prior: bfloat16 [2048, 16, 128, 128], P('rows', 'cols'), may hold values from -6 to 6
- candidates: int32 [2048, 16], P('rows', 'cols'), may hold values from 0 to 2047, as said below
- cross_link: int32 [2048], P(('rows', 'cols')), may hold values from 0 to 2047, as said below
- a1_blocks: bfloat16 [2048, 2, 128, 128], P(('rows', 'cols')), may hold values from -0.375 to 0.375
- a2_blocks: bfloat16 [2048, 128, 128], P(('rows', 'cols')), may hold values from -0.5 to 0.5
Outputs:
- similarity: bfloat16 [2048, 16, 128, 128], P('rows', 'cols')
Inputs may be any that keep to these rules, and one draw needn't show every extreme that they name: Target block t lies in target slab t // 16 and quarter (t // 4) % 4; a candidate in columns q * 4 to (q + 1) * 4 - 1 names a target of quarter q. The candidates of one row block in one quarter lie in distinct target slabs. Of the candidates held by one device, at most 1 lie in one target slab, and some slab gets exactly 1; every target slab gets 16 * 4 candidates of its quarter from all source slabs together. `cross_link`: the linked row block of a row block in slab r lies in the last half of the row blocks of slab (r + 1) % 128.
All inputs are finite; a program needn't handle non-finite values.
Results may differ from a plain program's by a relative error of at most 0.006.
Values may be sent and summed in bfloat16 or wider, within the bound.
A program may use at most 64 MiB of HBM per device.

v0:
```python
import jax
import jax.numpy as jnp
from jax import lax
from jax.sharding import PartitionSpec as P

mixing = 0.75


def passed_along(array, axis, by):
    count = lax.axis_size(axis)
    return lax.ppermute(array, axis, [(i, (i + by) % count) for i in range(count)])


def local(prior, candidates, cross_link, a1_blocks, a2_blocks):
    row_blocks = prior.shape[0]
    per_quarter = prior.shape[1]
    block = prior.shape[2]
    targets_here = a2_blocks.shape[0]
    slab_count = lax.axis_size("rows")
    column_count = lax.axis_size("cols")
    capacity = max(1, row_blocks * per_quarter // slab_count)
    upper_half = row_blocks // 2
    adjacency, links = (
        lax.all_gather(a1_blocks, "cols", axis=0, tiled=True),
        lax.all_gather(cross_link, "cols", axis=0, tiled=True),
    )
    within = links % row_blocks - upper_half
    next_ids = passed_along(candidates[upper_half:], "rows", -1)
    neighbour_ids = next_ids[within]
    matches = candidates[:, :, None] == neighbour_ids[:, None, :]
    chosen = jnp.sum(
        jnp.where(matches, jnp.arange(per_quarter, dtype=jnp.int32)[None, None, :], 0), axis=2
    )
    found = jnp.any(matches, axis=2)
    self_blocks = adjacency[:, 0]
    cross_blocks = adjacency[:, 1]

    def left_product(values):
        next_values = passed_along(values[upper_half:], "rows", -1)
        gathered = next_values[within]
        picked = jnp.take_along_axis(gathered, chosen[:, :, None, None], axis=1)
        picked = jnp.where(found[:, :, None, None], picked, jnp.zeros_like(picked))
        own_term = jnp.einsum(
            "ixy,ikyz->ikxz", self_blocks, values, preferred_element_type=jnp.float32
        )
        return own_term + jnp.einsum(
            "ixy,ikyz->ikxz", cross_blocks, picked, preferred_element_type=jnp.float32
        )

    flat_ids = candidates.reshape(-1)
    dest_slab = flat_ids // (column_count * targets_here)
    local_index = flat_ids % targets_here
    onehot = (dest_slab[:, None] == jnp.arange(slab_count, dtype=jnp.int32)[None, :]).astype(
        jnp.int32
    )
    running = jnp.cumsum(onehot, axis=0)
    dest_rank = jnp.sum(running * onehot, axis=1) - 1
    position = dest_slab * capacity + dest_rank
    requests = jnp.zeros((slab_count * capacity,), jnp.int32).at[position].set(local_index)
    wanted = lax.all_to_all(requests, "rows", split_axis=0, concat_axis=0, tiled=True)
    first = left_product(prior).astype(jnp.bfloat16)
    empty = jnp.zeros((slab_count * capacity, block, block), jnp.bfloat16)
    send_first = empty.at[position].set(first.reshape(-1, block, block))
    send_prior = empty.at[position].set(prior.reshape(-1, block, block))
    got_first, got_prior = (
        lax.all_to_all(send_first, "rows", split_axis=0, concat_axis=0, tiled=True),
        lax.all_to_all(send_prior, "rows", split_axis=0, concat_axis=0, tiled=True),
    )
    local_blocks = a2_blocks[wanted]
    image = jnp.einsum("sxy,szy->sxz", got_first, local_blocks, preferred_element_type=jnp.float32)
    swept = (mixing * image + (1.0 - mixing) * got_prior.astype(jnp.float32)).astype(jnp.bfloat16)
    product = jnp.einsum(
        "sxy,szy->sxz", swept, local_blocks, preferred_element_type=jnp.float32
    ).astype(jnp.bfloat16)
    returned = lax.all_to_all(product, "rows", split_axis=0, concat_axis=0, tiled=True)
    carried = returned[position].reshape(row_blocks, per_quarter, block, block)
    second = left_product(carried)
    return (mixing * second + (1.0 - mixing) * prior.astype(jnp.float32)).astype(jnp.bfloat16)


def solution(mesh):
    placed = (
        P("rows", "cols", None, None),
        P("rows", "cols"),
        P(("rows", "cols")),
        P(("rows", "cols"), None, None, None),
        P(("rows", "cols"), None, None),
    )
    return jax.shard_map(
        local, mesh=mesh, in_specs=placed, out_specs=P("rows", "cols", None, None), check_vma=False
    )
```

profile of v0, /device:TPU:1, one launch (start us, length us, event | category | flops | bytes accessed | tf_op | source)
XLA Modules:
  0.0 745.1 jit_solution(7629162179068298504)
XLA Ops:
  9.4 20.6 %all-to-all-start.1 = ((s32[128,1,1]{2,1,0:T(1,128)}), s32[128,1,1]{2,1,0:T(1,128)S(1)}, u32[]{:S(2)}, u32[]{:S(2)}) async-start(s32[128,1,1]{2,1,0:T(1,128)} %copy.83), calls=%async_computation.1 | async-start | bytes 131072 | tf_op jit(solution)/shard_map/all_to_all | solution.py:60
  30.0 3.0 broadcast_in_dim.35.clone
  33.0 8.7 %scatter_fusion.1 = bf16[128,128,128]{2,1,0:T(8,128)(2,1)} fusion(bf16[128,128,128]{2,1,0:T(8,128)(2,1)} %broadcast_in_dim.35.clone, s32[64]{0:T(128)S(1)} %fusion.20, bf16[64,128,128]{2,1,0:T(8,128)(2,1)S(1)} %bitcast.57), kind=kCustom, calls=%fused_computation.9 | custom fusion | bytes 6291712 | tf_op jit(solution)/shard_map/scatter | solution.py:64
  41.7 3.2 all-to-all-done.1
  45.0 13.6 %all-to-all-start.2 = ((bf16[128,128,128]{2,1,0:T(8,128)(2,1)}), bf16[128,128,128]{2,1,0:T(8,128)(2,1)}, u32[]{:S(2)}, u32[]{:S(2)}) async-start(bf16[128,128,128]{2,1,0:T(8,128)(2,1)} %scatter_fusion.1), calls=%async_computation.2 | async-start | bytes 8388608 | tf_op jit(solution)/shard_map/all_to_all | solution.py:67
  60.5 2.9 collective-permute-start.1
  63.4 6.8 collective-permute-start
  72.3 7.6 %all-reduce = s32[16]{0:T(128)S(1)} all-reduce(s32[16]{0:T(128)S(1)} %dynamic-update-slice), channel_id=1, replica_groups=mesh['rows'=128,'cols'=4] {'cols'}, use_global_device_ids=true, to_apply=%add | all-reduce | flops 16 | bytes 128
  79.9 170.9 %collective-permute-done = s32[8,4]{1,0:T(8,128)S(1)} collective-permute-done((s32[8,4]{1,0:T(8,128)S(1)}, s32[8,4]{1,0:T(8,128)S(1)}, u32[]{:S(2)}, u32[]{:S(2)}) %collective-permute-start) | collective-permute-done | bytes 160 | tf_op jit(solution)/shard_map/ppermute | solution.py:11
  251.9 2.1 gather_fusion.1
  254.0 3.8 gather_fusion.5
  257.8 3.9 copy.81
  265.9 4.1 copy.82
  269.9 3.0 broadcast_in_dim.35.clone.1
  272.9 10.0 %scatter_fusion = bf16[128,128,128]{2,1,0:T(8,128)(2,1)} fusion(bf16[128,128,128]{2,1,0:T(8,128)(2,1)} %broadcast_in_dim.35.clone.1, s32[64]{0:T(128)S(1)} %fusion.20, bf16[64,128,128]{2,1,0:T(8,128)(2,1)} %copy.82), kind=kCustom, calls=%fused_computation.7 | custom fusion | bytes 6291712 | tf_op jit(solution)/shard_map/scatter | solution.py:63
  283.0 15.3 %all-to-all-start = ((bf16[128,128,128]{2,1,0:T(8,128)(2,1)}), bf16[128,128,128]{2,1,0:T(8,128)(2,1)}, u32[]{:S(2)}, u32[]{:S(2)}) async-start(bf16[128,128,128]{2,1,0:T(8,128)(2,1)} %scatter_fusion), calls=%async_computation | async-start | bytes 8388608 | tf_op jit(solution)/shard_map/all_to_all | solution.py:66
  298.2 2.4 reduce
  300.6 3.1 gather_fusion.2
  303.7 180.0 %all-to-all-done = bf16[128,128,128]{2,1,0:T(8,128)(2,1)} async-done(((bf16[128,128,128]{2,1,0:T(8,128)(2,1)}), bf16[128,128,128]{2,1,0:T(8,128)(2,1)}, u32[]{:S(2)}, u32[]{:S(2)}) %all-to-all-start) | async-done | bytes 4194336 | tf_op jit(solution)/shard_map/all_to_all | solution.py:66
  483.7 13.2 %fusion.6 = bf16[128,128,128]{2,1,0:T(8,128)(2,1)} fusion(bf16[128,128,128]{2,1,0:T(8,128)(2,1)} %gather_fusion.2, bf16[128,128,128]{2,1,0:T(8,128)(2,1)} %all-to-all-done.2, bf16[128,128,128]{2,1,0:T(8,128)(2,1)} %all-to-all-done), kind=kOutput, calls=%fused_computation.18 | convolution fusion | flops 1086324736 | bytes 16777216 | tf_op jit(solution)/shard_map/sxy,szy->sxz/dot_general | solution.py:72
  496.9 12.4 %all-to-all-start.3 = ((bf16[128,128,128]{2,1,0:T(8,128)(2,1)}), bf16[128,128,128]{2,1,0:T(8,128)(2,1)}, u32[]{:S(2)}, u32[]{:S(2)}) async-start(bf16[128,128,128]{2,1,0:T(8,128)(2,1)} %fusion.6), calls=%async_computation.3 | async-start | bytes 8388608 | tf_op jit(solution)/shard_map/all_to_all | solution.py:75
  509.3 185.4 %all-to-all-done.3 = bf16[128,128,128]{2,1,0:T(8,128)(2,1)} async-done(((bf16[128,128,128]{2,1,0:T(8,128)(2,1)}), bf16[128,128,128]{2,1,0:T(8,128)(2,1)}, u32[]{:S(2)}, u32[]{:S(2)}) %all-to-all-start.3) | async-done | bytes 4194336 | tf_op jit(solution)/shard_map/all_to_all | solution.py:75
  694.7 4.3 gather_fusion.3
  699.1 2.3 slice.41
  701.4 4.2 collective-permute-start.2
  705.6 2.6 copy.88
  708.2 4.4 fusion.15
  712.5 8.5 %collective-permute-done.2 = bf16[8,4,128,128]{3,2,1,0:T(8,128)(2,1)S(1)} collective-permute-done((bf16[8,4,128,128]{3,2,1,0:T(8,128)(2,1)}, bf16[8,4,128,128]{3,2,1,0:T(8,128)(2,1)S(1)}, u32[]{:S(2)}, u32[]{:S(2)}) %collective-permute-start.2) | collective-permute-done | bytes 1048608 | tf_op jit(solution)/shard_map/ppermute | solution.py:11
  722.0 2.2 gather_fusion.6
  724.1 4.2 copy.87
  728.3 6.0 fusion.1
  734.3 3.9 copy.89
  (57 shorter events, 12.5 us)
Async XLA Ops:
  6.5 294.1 %copy-start = (bf16[4,128,128]{2,1,0:T(8,128)(2,1)S(1)}, bf16[4,128,128]{2,1,0:T(8,128)(2,1)}, u32[]{:S(2)}) copy-start(bf16[4,128,128]{2,1,0:T(8,128)(2,1)} %param.11) | copy-start | bytes 393220
  9.4 35.5 %all-to-all-start.1 = ((s32[128,1,1]{2,1,0:T(1,128)}), s32[128,1,1]{2,1,0:T(1,128)S(1)}, u32[]{:S(2)}, u32[]{:S(2)}) async-start(s32[128,1,1]{2,1,0:T(1,128)} %copy.83), calls=%async_computation.1 | async-start | bytes 131072 | tf_op jit(solution)/shard_map/all_to_all | solution.py:60
  30.0 3.0 copy-start.2
  41.7 16.9 %copy-start.6 = (bf16[4,2,128,128]{3,2,1,0:T(8,128)(2,1)S(1)}, bf16[4,2,128,128]{3,2,1,0:T(8,128)(2,1)}, u32[]{:S(2)}) copy-start(bf16[4,2,128,128]{3,2,1,0:T(8,128)(2,1)} %param.10) | copy-start | bytes 786436
  45.0 238.0 %all-to-all-start.2 = ((bf16[128,128,128]{2,1,0:T(8,128)(2,1)}), bf16[128,128,128]{2,1,0:T(8,128)(2,1)}, u32[]{:S(2)}, u32[]{:S(2)}) async-start(bf16[128,128,128]{2,1,0:T(8,128)(2,1)} %scatter_fusion.1), calls=%async_computation.2 | async-start | bytes 8388608 | tf_op jit(solution)/shard_map/all_to_all | solution.py:67
  58.5 13.5 %copy-start.8 = (s32[4]{0:T(128)S(1)}, s32[4]{0:T(128)}, u32[]{:S(2)}) copy-start(s32[4]{0:T(128)} %param.9) | copy-start | bytes 52
  58.6 192.9 %copy-start.7 = (s32[16,4]{0,1:T(4,128)S(1)}, s32[16,4]{0,1:T(4,128)}, u32[]{:S(2)}) copy-start(s32[16,4]{0,1:T(4,128)} %param.8) | copy-start | bytes 772
  58.6 203.2 %all-gather.2.cloned.1.call-start = ((), (), s32[]{:S(2)}) async-start(), calls=%async_computation.4 | async-start | bytes 1310720 | tf_op jit(solution)/shard_map/all_gather | solution.py:24
  60.5 191.4 %collective-permute-start.1 = (bf16[8,4,128,128]{3,2,1,0:T(8,128)(2,1)}, bf16[8,4,128,128]{3,2,1,0:T(8,128)(2,1)S(1)}, u32[]{:S(2)}, u32[]{:S(2)}) collective-permute-start(bf16[8,4,128,128]{3,2,1,0:T(8,128)(2,1)} %slice.20), channel_id=1, source_target_pairs={{0,508},{4,0},{8,4},{12,8},{16,12},{20,16},{24,20},{28,24},{32,28}... | collective-permute-start | bytes 3145736 | tf_op jit(solution)/shard_map/ppermute | solution.py:11
  63.4 187.4 %collective-permute-start = (s32[8,4]{1,0:T(8,128)S(1)}, s32[8,4]{1,0:T(8,128)S(1)}, u32[]{:S(2)}, u32[]{:S(2)}) collective-permute-start(s32[8,4]{1,0:T(8,128)S(1)} %slice.39), channel_id=1, source_target_pairs={{0,508},{4,0},{8,4},{12,8},{16,12},{20,16},{24,20},{28,24},{32,28}... | collective-permute-start | bytes 392 | tf_op jit(solution)/shard_map/ppermute | solution.py:11
  261.8 2.0 copy-start.3
  261.8 2.0 copy-start.4
  283.0 200.7 %all-to-all-start = ((bf16[128,128,128]{2,1,0:T(8,128)(2,1)}), bf16[128,128,128]{2,1,0:T(8,128)(2,1)}, u32[]{:S(2)}, u32[]{:S(2)}) async-start(bf16[128,128,128]{2,1,0:T(8,128)(2,1)} %scatter_fusion), calls=%async_computation | async-start | bytes 8388608 | tf_op jit(solution)/shard_map/all_to_all | solution.py:66
  496.9 197.8 %all-to-all-start.3 = ((bf16[128,128,128]{2,1,0:T(8,128)(2,1)}), bf16[128,128,128]{2,1,0:T(8,128)(2,1)}, u32[]{:S(2)}, u32[]{:S(2)}) async-start(bf16[128,128,128]{2,1,0:T(8,128)(2,1)} %fusion.6), calls=%async_computation.3 | async-start | bytes 8388608 | tf_op jit(solution)/shard_map/all_to_all | solution.py:75
  701.4 19.6 %collective-permute-start.2 = (bf16[8,4,128,128]{3,2,1,0:T(8,128)(2,1)}, bf16[8,4,128,128]{3,2,1,0:T(8,128)(2,1)S(1)}, u32[]{:S(2)}, u32[]{:S(2)}) collective-permute-start(bf16[8,4,128,128]{3,2,1,0:T(8,128)(2,1)} %bitcast.20), channel_id=1, source_target_pairs={{0,508},{4,0},{8,4},{12,8},{16,12},{20,16},{24,20},{28,24},{32,28}... | collective-permute-start | bytes 3145736 | tf_op jit(solution)/shard_map/ppermute | solution.py:11
  724.1 4.2 copy-start.5
  728.3 9.9 %copy-start.1 = (bf16[4,128,128]{2,1,0:T(8,128)(2,1)S(1)}, bf16[4,128,128]{2,1,0:T(8,128)(2,1)}, u32[]{:S(2)}) copy-start(bf16[4,128,128]{2,1,0:T(8,128)(2,1)} %param.11) | copy-start | bytes 393220
Sparse Core Ops, SparseCore 0:
  61.5 30.7 all-gather.1
where the time goes:
time: 746 us; the launch traced here: 745 us
  waiting for transfers between devices  548 us (73%)
  starting transfers between devices  75.6 us (10%)
  local copies, waits for them, and re-layouts  69.1 us (9%)
  matrix products  27.6 us (4%)
  between operations  14.3 us (2%)
  blocking collectives  7.57 us (1%)
    all_to_all x1, waiting for transfers between devices, local(): lax.all_to_all(product, 'rows', split_axis=0, concat_axis=0, tiled=True)  185 us
    all_to_all x1, waiting for transfers between devices, local(): lax.all_to_all(send_first, 'rows', split_axis=0, concat_axis=0, tiled=True)  180 us
    ppermute x3, waiting for transfers between devices, passed_along(): lax.ppermute(array, axis, [(i, (i + by) % count) for i in range(count)])  179 us
    all_to_all x1, starting transfers between devices, local(): lax.all_to_all(requests, 'rows', split_axis=0, concat_axis=0, tiled=True)  20.6 us
    all_to_all x1, starting transfers between devices, local(): lax.all_to_all(send_first, 'rows', split_axis=0, concat_axis=0, tiled=True)  15.3 us
  transfers between devices with their start and end apart: 8, of which 5 were waited for; matrix products, arithmetic and copies ran while one was open for 8% of the time, Pallas kernels for 0%

commit v1 on v0

v1 whole, which is shorter than its diff:
```python
import jax
import jax.numpy as jnp
from jax import lax
from jax.experimental import pallas as pl
from jax.experimental.pallas import tpu as pltpu
from jax.sharding import PartitionSpec as P

mixing = 0.75


def passed_along(array, axis, by):
    count = lax.axis_size(axis)
    return lax.ppermute(array, axis, [(i, (i + by) % count) for i in range(count)])


def contract(a, b, dims):
    return lax.dot_general(a, b, (dims, ((), ())), preferred_element_type=jnp.float32)


def left_kernel(within, chosen, found, prior, next_prior, adjacency, first):
    rows, per = prior.shape[0], prior.shape[1]

    def step(i, carry):
        for k in range(per):
            n = i * per + k
            picked = next_prior[within[i], chosen[n]]
            picked = jnp.where(found[n] > 0, picked, jnp.zeros_like(picked))
            total = contract(adjacency[i, 0], prior[i, k], ((1,), (0,)))
            total = total + contract(adjacency[i, 1], picked, ((1,), (0,)))
            first[i, k] = total.astype(jnp.bfloat16)
        return carry

    lax.fori_loop(0, rows, step, 0)


def sweep_kernel(
    within, chosen, found, place, prior, next_prior, first, next_first, adjacency, a2, out, blocks, sems
):
    rows, per = prior.shape[0], prior.shape[1]

    def fetch(n):
        return pltpu.make_async_copy(a2.at[place[n]], blocks.at[n], sems.at[n])

    def begin(n, carry):
        fetch(n).start()
        return carry

    lax.fori_loop(0, rows * per, begin, 0)

    def step(i, carry):
        for k in range(per):
            fetch(i * per + k).wait()
        for k in range(per):
            n = i * per + k
            keep = found[n] > 0
            picked_prior = next_prior[within[i], chosen[n]]
            picked_first = next_first[within[i], chosen[n]]
            zero = jnp.zeros_like(picked_prior)
            picked_prior = jnp.where(keep, picked_prior, zero)
            picked_first = jnp.where(keep, picked_first, zero)
            own_prior = prior[i, k]
            target = blocks[n]
            values = jnp.concatenate([first[i, k], picked_first], axis=0)
            base = jnp.concatenate([own_prior, picked_prior], axis=0).astype(jnp.float32)
            image = contract(values, target, ((1,), (1,)))
            swept = (mixing * image + (1.0 - mixing) * base).astype(jnp.bfloat16)
            carried = contract(swept, target, ((1,), (1,))).astype(jnp.bfloat16)
            block = own_prior.shape[0]
            total = contract(adjacency[i, 0], carried[:block], ((1,), (0,)))
            total = total + contract(adjacency[i, 1], carried[block:], ((1,), (0,)))
            out[i, k] = (mixing * total + (1.0 - mixing) * own_prior.astype(jnp.float32)).astype(
                jnp.bfloat16
            )
        return carry

    lax.fori_loop(0, rows, step, 0)


def local(prior, candidates, cross_link, a1_blocks, a2_blocks):
    row_blocks, per_quarter, block = prior.shape[0], prior.shape[1], prior.shape[2]
    targets_here = a2_blocks.shape[0]
    column_count = lax.axis_size("cols")
    upper_half = row_blocks // 2
    smem = pl.BlockSpec(memory_space=pltpu.SMEM)
    vmem = pl.BlockSpec(memory_space=pltpu.VMEM)
    adjacency = lax.all_gather(a1_blocks, "cols", axis=0, tiled=True)
    links = lax.all_gather(cross_link, "cols", axis=0, tiled=True)
    targets = lax.all_gather(a2_blocks, "rows", axis=0, tiled=True)
    within = links % row_blocks - upper_half
    next_ids = passed_along(candidates[upper_half:], "rows", -1)
    next_prior = passed_along(prior[upper_half:], "rows", -1)
    matches = candidates[:, :, None] == next_ids[within][:, None, :]
    chosen = jnp.sum(
        jnp.where(matches, jnp.arange(per_quarter, dtype=jnp.int32)[None, None, :], 0), axis=2
    ).reshape(-1)
    found = jnp.any(matches, axis=2).astype(jnp.int32).reshape(-1)
    place = (
        candidates // (column_count * targets_here) * targets_here + candidates % targets_here
    ).reshape(-1)
    shape = jax.ShapeDtypeStruct(prior.shape, jnp.bfloat16)
    flops = 2 * row_blocks * per_quarter * block**3
    first = pl.pallas_call(
        left_kernel,
        out_shape=shape,
        in_specs=[smem, smem, smem, vmem, vmem, vmem],
        out_specs=vmem,
        cost_estimate=pl.CostEstimate(
            flops=2 * flops, bytes_accessed=4 * prior.size * 2, transcendentals=0
        ),
    )(within, chosen, found, prior, next_prior, adjacency)
    next_first = passed_along(first[upper_half:], "rows", -1)
    return pl.pallas_call(
        sweep_kernel,
        out_shape=shape,
        in_specs=[smem] * 4 + [vmem] * 5 + [pl.BlockSpec(memory_space=pl.ANY)],
        out_specs=vmem,
        scratch_shapes=[
            pltpu.VMEM((row_blocks * per_quarter, block, block), jnp.bfloat16),
            pltpu.SemaphoreType.DMA((row_blocks * per_quarter,)),
        ],
        cost_estimate=pl.CostEstimate(
            flops=6 * flops, bytes_accessed=6 * prior.size * 2, transcendentals=0
        ),
    )(within, chosen, found, place, prior, next_prior, first, next_first, adjacency, targets)


def solution(mesh):
    placed = (
        P("rows", "cols", None, None),
        P("rows", "cols"),
        P(("rows", "cols")),
        P(("rows", "cols"), None, None, None),
        P(("rows", "cols"), None, None),
    )
    return jax.shard_map(
        local, mesh=mesh, in_specs=placed, out_specs=P("rows", "cols", None, None), check_vma=False
    )
```

time: 746 us -> 237 us (0.32)
  waiting for transfers between devices: 548 us -> 157 us
  local copies, waits for them, and re-layouts: 69.1 us -> 7.06 us
  starting transfers between devices: 75.6 us -> 21.5 us
  Pallas kernels: 0 us -> 29 us
  matrix products: 27.6 us -> 0 us
    all_to_all x4 -> x0, waiting for transfers between devices: 369 us -> none  [the longest x1 185 us: local(): lax.all_to_all(product, 'rows', split_axis=0, concat_axis=0, tiled=True)]
    ppermute x3, waiting for transfers between devices: 179 us -> 14 us  [passed_along(): lax.ppermute(array, axis, [(i, (i + by) % count) for i in range(count)])]
    all_gather x1 -> x2, waiting for transfers between devices: 0.01 us -> 142 us  [the longest x1 136 us: local(): targets = lax.all_gather(a2_blocks, 'rows', axis=0, tiled=True)]
    all_to_all x4 -> x0, starting transfers between devices: 61.8 us -> none  [the longest x1 20.6 us: local(): lax.all_to_all(requests, 'rows', split_axis=0, concat_axis=0, tiled=True)]
    pallas_call x0 -> x2, Pallas kernels: none -> 29 us  [the longest x1 21.9 us: local(): pl.pallas_call(sweep_kernel, out_shape=shape, in_specs=[smem] * 4 + [vmem...]
    dot_general x5 -> x0, matrix products: 27.6 us -> none  [the longest x1 13.2 us: local(): jnp.einsum('sxy,szy->sxz', swept, local_blocks, preferred_element_type=jn...]
    gather x12 -> x2, local copies, waits for them, and re-layouts: 25.3 us -> 0.64 us  [local(): matches = candidates[:, :, None] == next_ids[within][:, None, :]]
    scatter x3 -> x0, local copies, waits for them, and re-layouts: 19.5 us -> none  [the longest x1 10 us: local(): send_first = empty.at[position].set(first.reshape(-1, block, block))]
  transfers between devices with their start and end apart: 8 -> 5, of which waited for: 5 -> 3; matrix products, arithmetic and copies ran while one was open for 8% -> 3% of each run, Pallas kernels for 0% -> 3%
where the time goes in v1:
time: 237 us
  waiting for transfers between devices  157 us (66%)
  Pallas kernels  29 us (12%)
  starting transfers between devices  21.5 us (9%)
  between operations  14.2 us (6%)
  local copies, waits for them, and re-layouts  7.06 us (3%)
  blocking collectives  6.86 us (3%)
    all_gather x1, waiting for transfers between devices, local(): targets = lax.all_gather(a2_blocks, 'rows', axis=0, tiled=True)  136 us
    pallas_call x1, Pallas kernels, local(): pl.pallas_call(sweep_kernel, out_shape=shape, in_specs=[smem] * 4 + [vmem...  21.9 us
    ppermute x3, starting transfers between devices, passed_along(): lax.ppermute(array, axis, [(i, (i + by) % count) for i in range(count)])  21.4 us
    ppermute x3, waiting for transfers between devices, passed_along(): lax.ppermute(array, axis, [(i, (i + by) % count) for i in range(count)])  14 us
    pallas_call x1, Pallas kernels, local(): pl.pallas_call(left_kernel, out_shape=shape, in_specs=[smem, smem, smem,...  7.13 us
    unnamed x1, blocking collectives  6.86 us
    all_gather x1, waiting for transfers between devices, local(): adjacency = lax.all_gather(a1_blocks, 'cols', axis=0, tiled=True)  6.47 us
  transfers between devices with their start and end apart: 5, of which 3 were waited for; matrix products, arithmetic and copies ran while one was open for 3% of the time, Pallas kernels for 3%

profile of v1, /device:TPU:1, one launch (start us, length us, event | category | flops | bytes accessed | tf_op | source)
XLA Modules:
  0.0 236.5 jit_solution(12745605479804520829)
XLA Ops:
  6.5 0.0 all-gather.3.cloned.1.call-start
  6.5 0.7 all-gather.3.cloned.1.call-update
  7.3 0.0 all-gather.5.cloned.1.call-start
  7.3 0.7 all-gather.5.cloned.1.call-update
  8.0 1.3 slice.10
  9.3 8.7 %collective-permute-start.1 = (bf16[8,4,128,128]{3,2,1,0:T(8,128)(2,1)S(1)}, bf16[8,4,128,128]{3,2,1,0:T(8,128)(2,1)S(1)}, u32[]{:S(2)}, u32[]{:S(2)}) collective-permute-start(bf16[8,4,128,128]{3,2,1,0:T(8,128)(2,1)S(1)} %slice.10), channel_id=1, source_target_pairs={{0,508},{4,0},{8,4},{12,8},{16,12},{20,16},{24,20},{28,24},{32,28}... | collective-permute-start | bytes 3145736 | tf_op jit(solution)/shard_map/ppermute | solution.py:13
  18.1 0.0 copy-done.2
  18.1 0.1 slice.9
  18.1 0.1 copy.20
  18.2 7.9 %collective-permute-start = (s32[8,4]{1,0:T(8,128)S(1)}, s32[8,4]{1,0:T(8,128)S(1)}, u32[]{:S(2)}, u32[]{:S(2)}) collective-permute-start(s32[8,4]{1,0:T(8,128)S(1)} %copy.20), channel_id=1, source_target_pairs={{0,508},{4,0},{8,4},{12,8},{16,12},{20,16},{24,20},{28,24},{32,28}... | collective-permute-start | bytes 392 | tf_op jit(solution)/shard_map/ppermute | solution.py:13
  26.2 1.3 dynamic-slice
  28.1 0.0 copy-done.3
  28.1 0.2 dynamic-update-slice
  28.4 6.9 %all-reduce = s32[16]{0:T(128)S(1)} all-reduce(s32[16]{0:T(128)S(1)} %dynamic-update-slice), channel_id=1, replica_groups=mesh['rows'=128,'cols'=4] {'cols'}, use_global_device_ids=true, to_apply=%add | all-reduce | flops 16 | bytes 128
  35.2 0.5 broadcast_add_fusion.within
  35.8 0.0 collective-permute-done
  35.8 0.6 gather_fusion
  36.4 0.1 copy.16
  36.5 0.1 copy.18
  36.6 0.7 reshape.14.found
  37.3 0.1 copy.17
  37.4 0.6 reshape.12.chosen
  38.0 0.0 collective-permute-done.1.next_prior
  38.0 6.5 %all-gather.3.cloned.1.call-done.adjacency = bf16[16,2,128,128]{3,2,1,0:T(8,128)(2,1)} async-done(((bf16[4,2,128,128]{3,2,1,0:T(8,128)(2,1)}), bf16[16,2,128,128]{3,2,1,0:T(8,128)(2,1)}) %all-gather.3.cloned.1.call-update) | async-done | bytes 1048592 | tf_op jit(solution)/shard_map/all_gather | solution.py:86
  44.4 7.1 %shard_map.55.first = bf16[16,4,128,128]{3,2,1,0:T(8,128)(2,1)} custom-call(s32[16]{0:T(128)} %broadcast_add_fusion.within, s32[64]{0:T(128)} %reshape.12.chosen, s32[64]{0:T(128)} %reshape.14.found, bf16[16,4,128,128]{3,2,1,0:T(8,128)(2,1)} %prior.3, bf16[8,4,128,128]{3,2,1,0:T(8,128)(2,1)} %copy-done, ...), custom_call_target="tpu_custom_call" | custom-call | flops 536870912 | bytes 8388608 | tf_op jit(solution)/shard_map/pallas_call | solution.py:102
  51.6 1.3 slice.14
  52.9 4.7 %collective-permute-start.2 = (bf16[8,4,128,128]{3,2,1,0:T(8,128)(2,1)S(1)}, bf16[8,4,128,128]{3,2,1,0:T(8,128)(2,1)S(1)}, u32[]{:S(2)}, u32[]{:S(2)}) collective-permute-start(bf16[8,4,128,128]{3,2,1,0:T(8,128)(2,1)S(1)} %slice.14), channel_id=1, source_target_pairs={{0,508},{4,0},{8,4},{12,8},{16,12},{20,16},{24,20},{28,24},{32,28}... | collective-permute-start | bytes 3145736 | tf_op jit(solution)/shard_map/ppermute | solution.py:13
  57.6 0.1 copy.19
  57.7 0.6 reshape.13.place
  58.3 13.9 %collective-permute-done.2.next_first = bf16[8,4,128,128]{3,2,1,0:T(8,128)(2,1)S(1)} collective-permute-done((bf16[8,4,128,128]{3,2,1,0:T(8,128)(2,1)S(1)}, bf16[8,4,128,128]{3,2,1,0:T(8,128)(2,1)S(1)}, u32[]{:S(2)}, u32[]{:S(2)}) %collective-permute-start.2) | collective-permute-done | bytes 1048608 | tf_op jit(solution)/shard_map/ppermute | solution.py:13
  72.3 135.5 %all-gather.5.cloned.1.call-done.a2 = bf16[512,128,128]{2,1,0:T(8,128)(2,1)} async-done(((bf16[4,128,128]{2,1,0:T(8,128)(2,1)}), bf16[512,128,128]{2,1,0:T(8,128)(2,1)}) %all-gather.5.cloned.1.call-update) | async-done | bytes 16777232 | tf_op jit(solution)/shard_map/all_gather | solution.py:88
  207.8 21.9 %shard_map.56 = bf16[16,4,128,128]{3,2,1,0:T(8,128)(2,1)} custom-call(s32[16]{0:T(128)} %broadcast_add_fusion.within, s32[64]{0:T(128)} %reshape.12.chosen, s32[64]{0:T(128)} %reshape.14.found, s32[64]{0:T(128)} %reshape.13.place, bf16[16,4,128,128]{3,2,1,0:T(8,128)(2,1)} %prior.3, bf16[8,4,128,128]{3,2,1,0:T(8,128)(2,1)} %copy-done, ...), custom_call_target="tpu_custom_call" | custom-call | flops 1610612736 | bytes 12582912 | tf_op jit(solution)/shard_map/pallas_call | solution.py:112
  (13 shorter events, 0.1 us)
Async XLA Ops:
  6.5 11.5 %copy-start.2 = (s32[16,4]{0,1:T(4,128)S(1)}, s32[16,4]{0,1:T(4,128)}, u32[]{:S(2)}) copy-start(s32[16,4]{0,1:T(4,128)} %param.6) | copy-start | bytes 772
  6.5 21.6 %copy-start.3 = (s32[4]{0:T(128)S(1)}, s32[4]{0:T(128)}, u32[]{:S(2)}) copy-start(s32[4]{0:T(128)} %param.7) | copy-start | bytes 52
  6.5 37.9 %all-gather.3.cloned.1.call-start = ((), (), s32[]{:S(2)}) async-start(), calls=%async_computation | async-start | bytes 1310720 | tf_op jit(solution)/shard_map/all_gather | solution.py:86
  7.3 200.5 %all-gather.5.cloned.1.call-start = ((), (), s32[]{:S(2)}) async-start(), calls=%async_computation.1 | async-start | bytes 16908288 | tf_op jit(solution)/shard_map/all_gather | solution.py:88
  9.3 28.7 %collective-permute-start.1 = (bf16[8,4,128,128]{3,2,1,0:T(8,128)(2,1)S(1)}, bf16[8,4,128,128]{3,2,1,0:T(8,128)(2,1)S(1)}, u32[]{:S(2)}, u32[]{:S(2)}) collective-permute-start(bf16[8,4,128,128]{3,2,1,0:T(8,128)(2,1)S(1)} %slice.10), channel_id=1, source_target_pairs={{0,508},{4,0},{8,4},{12,8},{16,12},{20,16},{24,20},{28,24},{32,28}... | collective-permute-start | bytes 3145736 | tf_op jit(solution)/shard_map/ppermute | solution.py:13
  18.2 17.6 %collective-permute-start = (s32[8,4]{1,0:T(8,128)S(1)}, s32[8,4]{1,0:T(8,128)S(1)}, u32[]{:S(2)}, u32[]{:S(2)}) collective-permute-start(s32[8,4]{1,0:T(8,128)S(1)} %copy.20), channel_id=1, source_target_pairs={{0,508},{4,0},{8,4},{12,8},{16,12},{20,16},{24,20},{28,24},{32,28}... | collective-permute-start | bytes 392 | tf_op jit(solution)/shard_map/ppermute | solution.py:13
  38.0 6.5 %copy-start = (bf16[8,4,128,128]{3,2,1,0:T(8,128)(2,1)}, bf16[8,4,128,128]{3,2,1,0:T(8,128)(2,1)S(1)}, u32[]{:S(2)}) copy-start(bf16[8,4,128,128]{3,2,1,0:T(8,128)(2,1)S(1)} %collective-permute-done.1.next_prior) | copy-start | bytes 3145732
  52.9 19.4 %collective-permute-start.2 = (bf16[8,4,128,128]{3,2,1,0:T(8,128)(2,1)S(1)}, bf16[8,4,128,128]{3,2,1,0:T(8,128)(2,1)S(1)}, u32[]{:S(2)}, u32[]{:S(2)}) collective-permute-start(bf16[8,4,128,128]{3,2,1,0:T(8,128)(2,1)S(1)} %slice.14), channel_id=1, source_target_pairs={{0,508},{4,0},{8,4},{12,8},{16,12},{20,16},{24,20},{28,24},{32,28}... | collective-permute-start | bytes 3145736 | tf_op jit(solution)/shard_map/ppermute | solution.py:13
  72.3 135.5 %copy-start.1 = (bf16[8,4,128,128]{3,2,1,0:T(8,128)(2,1)}, bf16[8,4,128,128]{3,2,1,0:T(8,128)(2,1)S(1)}, u32[]{:S(2)}) copy-start(bf16[8,4,128,128]{3,2,1,0:T(8,128)(2,1)S(1)} %collective-permute-done.2.next_first) | copy-start | bytes 3145732
Sparse Core Ops, SparseCore 0:
  9.4 34.9 all-gather.2
  47.6 160.1 all-gather.4

commit v2 on v1

--- a/solution.py
+++ b/solution.py
@@ -75,6 +75,214 @@
 
     lax.fori_loop(0, rows, step, 0)
 
+MESH = pl.DeviceIdType.MESH
+ny, nz, cores = 4, 16, 2
+
+
+def gather_kernel(
+    a2, whole, own_sem, az_s, az_r, bz_s, bz_r, by_s, by_r, ay_s, ay_r, ah_s, ah_r, sib_s, sib_r
+):
+    me, col = lax.axis_index("rows"), lax.axis_index("cols")
+    core = lax.rem(me, cores)
+    z = lax.rem(me // cores, nz)
+    y = me // (cores * nz)
+    height = a2.shape[0]
+    cut = height * 5 // 8
+    a_half, b_half = cut // 2, (height - cut) // 2
+    a_all, b_all = pl.ds(0, cut), pl.ds(cut, height - cut)
+    a_part = (pl.ds(0, a_half), pl.ds(a_half, a_half))
+    b_part = (pl.ds(cut, b_half), pl.ds(cut + b_half, b_half))
+
+    def zz(by):
+        return lax.rem(z + by + nz, nz)
+
+    def yy(by):
+        return lax.rem(y + by + ny, ny)
+
+    def device(y_at, z_at, core_at):
+        return ((y_at * nz + z_at) * cores + core_at, col)
+
+    z_to = (device(y, zz(1), core), device(y, zz(-1), core))
+    y_to = (device(yy(1), z, core), device(yy(-1), z, core))
+    sibling = device(y, z, 1 - core)
+    sign = (-1, 1)
+
+    barrier = pltpu.get_barrier_semaphore()
+    for other in z_to + y_to + (sibling,):
+        pl.semaphore_signal(barrier, inc=1, device_id=other, device_id_type=MESH)
+    own = pltpu.make_async_copy(a2, whole.at[y, z, core], own_sem)
+    own.start()
+    pl.semaphore_wait(barrier, 5)
+
+    def copy(src, dst, send_sem, recv_sem, to):
+        return pltpu.make_async_remote_copy(
+            src_ref=src, dst_ref=dst, send_sem=send_sem, recv_sem=recv_sem,
+            device_id=to, device_id_type=MESH,
+        )
+
+    def az(d, s, part, mine=False):
+        place = whole.at[y, zz(sign[d] * (s - 1)), core, part]
+        return copy(a2.at[part] if mine else place, place, az_s.at[d, s], az_r.at[d, s], z_to[d])
+
+    def az_in(d, s, part):
+        place = whole.at[y, zz(sign[d] * s), core, part]
+        copy(place, place, az_s.at[d, s], az_r.at[d, s], z_to[d]).wait_recv()
+
+    def bz(d, s, part):
+        place = whole.at[:, zz(sign[d] * (s - 1)), core, part]
+        return copy(place, place, bz_s.at[d, s], bz_r.at[d, s], z_to[d])
+
+    def bz_in(d, s, part):
+        place = whole.at[:, zz(sign[d] * s), core, part]
+        copy(place, place, bz_s.at[d, s], bz_r.at[d, s], z_to[d]).wait_recv()
+
+    def by(d, h, y_at, part, mine=False):
+        place = whole.at[y_at, z, core, part]
+        return copy(a2.at[part] if mine else place, place, by_s.at[d, h], by_r.at[d, h], y_to[d])
+
+    def ay(d, z_at, mine=False):
+        place = whole.at[y, z_at, core, a_all]
+        return copy(a2.at[a_all] if mine else place, place, ay_s.at[d, z_at], ay_r.at[d, z_at], y_to[d])
+
+    def ay_in(d, z_at):
+        place = whole.at[yy(sign[d]), z_at, core, a_all]
+        copy(place, place, ay_s.at[d, z_at], ay_r.at[d, z_at], y_to[d]).wait_recv()
+
+    def ah(d, y_at, z_at):
+        place = whole.at[y_at, z_at, core, a_part[d]]
+        return copy(place, place, ah_s.at[d, z_at], ah_r.at[d, z_at], y_to[d])
+
+    def share(place):
+        copy(place, place, sib_s, sib_r, sibling).start()
+
+    def from_y(z_at):
+        for d in range(2):
+            ay_in(d, z_at)
+            ah(d, yy(sign[d]), z_at).start()
+            share(whole.at[yy(sign[d]), z_at, core, a_all])
+
+    def from_y_far(z_at):
+        for d in range(2):
+            ah(d, yy(2), z_at).wait_recv()
+        share(whole.at[yy(2), z_at, core, a_all])
+
+    def a_step(s, last):
+        for d in range(2):
+            z_at = zz(sign[d] * s)
+            az_in(d, s, a_all)
+            az(d, s + 1, a_part[d] if last else a_all).start()
+            for e in range(2):
+                ay(e, z_at).start()
+            share(whole.at[y, z_at, core, a_all])
+
+    def b_step(s, last):
+        for d in range(2):
+            z_at = zz(sign[d] * s)
+            bz_in(d, s, b_all)
+            bz(d, s + 1, b_part[d] if last else b_all).start()
+            share(whole.at[:, z_at, core, b_all])
+
+    for d in range(2):
+        az(d, 1, a_all, True).start()
+        by(d, 0, y, b_all, True).start()
+    for d in range(2):
+        ay(d, z, True).start()
+    for d in range(2):
+        by(d, 0, yy(sign[d]), b_all).wait_recv()
+        by(d, 1, yy(sign[d]), b_part[d]).start()
+    own.wait()
+    share(whole.at[y, z, core, a_all])
+    a_step(1, False)
+    for d in range(2):
+        by(d, 1, yy(2), b_part[d]).wait_recv()
+    for d in range(2):
+        bz(d, 1, b_all).start()
+    share(whole.at[:, z, core, b_all])
+    from_y(z)
+    a_step(2, False)
+    from_y_far(z)
+    for d in range(2):
+        from_y(zz(sign[d]))
+    b_step(1, False)
+
+    def steady(s, carry):
+        a_step(s, False)
+        for d in range(2):
+            from_y_far(zz(sign[d] * (s - 2)))
+        for d in range(2):
+            from_y(zz(sign[d] * (s - 1)))
+        b_step(s - 1, False)
+        return carry
+
+    far = nz // 2
+    lax.fori_loop(3, far - 1, steady, 0)
+    a_step(far - 1, True)
+    for d in range(2):
+        from_y_far(zz(sign[d] * (far - 3)))
+    for d in range(2):
+        from_y(zz(sign[d] * (far - 2)))
+    b_step(far - 2, False)
+    for d in range(2):
+        az_in(d, far, a_part[d])
+    for e in range(2):
+        ay(e, zz(far)).start()
+    share(whole.at[y, zz(far), core, a_all])
+    for d in range(2):
+        from_y_far(zz(sign[d] * (far - 2)))
+    for d in range(2):
+        from_y(zz(sign[d] * (far - 1)))
+    b_step(far - 1, True)
+    from_y(zz(far))
+    for d in range(2):
+        from_y_far(zz(sign[d] * (far - 1)))
+    for d in range(2):
+        bz_in(d, far, b_part[d])
+    share(whole.at[:, zz(far), core, b_all])
+    from_y_far(zz(far))
+
+    for d in range(2):
+        by(d, 0, y, b_all).wait_send()
+        by(d, 1, y, b_part[d]).wait_send()
+        az(d, far, a_part[d]).wait_send()
+        bz(d, far, b_part[d]).wait_send()
+
+    def sent_z(s, carry):
+        for d in range(2):
+            az(d, s, a_all).wait_send()
+            bz(d, s, b_all).wait_send()
+        return carry
+
+    lax.fori_loop(1, far, sent_z, 0)
+
+    def sent_y(z_at, carry):
+        for d in range(2):
+            ay(d, z_at).wait_send()
+            ah(d, y, z_at).wait_send()
+        return carry
+
+    lax.fori_loop(0, nz, sent_y, 0)
+    mine, theirs = whole.at[:, :, core], whole.at[:, :, 1 - core]
+    copy(mine, mine, sib_s, sib_r, sibling).wait_send()
+    copy(theirs, theirs, sib_s, sib_r, sibling).wait_recv()
+
+
+def gather_targets(a2_blocks):
+    targets_here, block = a2_blocks.shape[0], a2_blocks.shape[1]
+    height = targets_here * block
+    far = nz // 2
+    dma = pltpu.SemaphoreType.DMA
+    zs, ys = dma((2, far + 1)), dma((2, nz))
+    whole = pl.pallas_call(
+        gather_kernel,
+        out_shape=jax.ShapeDtypeStruct((ny, nz, cores, height, block), a2_blocks.dtype),
+        in_specs=[pl.BlockSpec(memory_space=pltpu.VMEM)],
+        out_specs=pl.BlockSpec(memory_space=pl.ANY),
+        scratch_shapes=[dma(())] + [zs] * 4 + [dma((2, 2))] * 2 + [ys] * 4 + [dma(())] * 2,
+        compiler_params=pltpu.CompilerParams(collective_id=0, has_side_effects=True),
+        cost_estimate=pl.CostEstimate(flops=0, bytes_accessed=150_000_000, transcendentals=0),
+    )(a2_blocks.reshape(height, block))
+    return whole.reshape(ny * nz * cores * targets_here, block, block)
+
 
 def local(prior, candidates, cross_link, a1_blocks, a2_blocks):
     row_blocks, per_quarter, block = prior.shape[0], prior.shape[1], prior.shape[2]
@@ -85,7 +293,7 @@
     vmem = pl.BlockSpec(memory_space=pltpu.VMEM)
     adjacency = lax.all_gather(a1_blocks, "cols", axis=0, tiled=True)
     links = lax.all_gather(cross_link, "cols", axis=0, tiled=True)
-    targets = lax.all_gather(a2_blocks, "rows", axis=0, tiled=True)
+    targets = gather_targets(a2_blocks)
     within = links % row_blocks - upper_half
     next_ids = passed_along(candidates[upper_half:], "rows", -1)
     next_prior = passed_along(prior[upper_half:], "rows", -1)

time: 237 us -> 166 us (0.70)
  waiting for transfers between devices: 157 us -> 7.99 us
  Pallas kernels: 29 us -> 107 us
    all_gather x1 -> x0, waiting for transfers between devices: 136 us -> none  [local(): targets = lax.all_gather(a2_blocks, 'rows', axis=0, tiled=True)]
    pallas_call x0 -> x1, Pallas kernels: none -> 77.9 us  [gather_targets(): pl.pallas_call(gather_kernel, out_shape=jax.ShapeDtypeStruct((ny, nz, cor...]
    ppermute x3, waiting for transfers between devices: 14 us -> 0.01 us  [passed_along(): lax.ppermute(array, axis, [(i, (i + by) % count) for i in range(count)])]
  transfers between devices with their start and end apart: 5 -> 4, of which waited for: 3 -> 1; matrix products, arithmetic and copies ran while one was open for 3% -> 4% of each run, Pallas kernels for 3% -> 47%
where the time goes in v2:
time: 166 us
  Pallas kernels  107 us (64%)
  starting transfers between devices  21.4 us (13%)
  between operations  14.2 us (9%)
  local copies, waits for them, and re-layouts  8.02 us (5%)
  waiting for transfers between devices  7.99 us (5%)
  blocking collectives  6.86 us (4%)
    pallas_call x1, Pallas kernels, gather_targets(): pl.pallas_call(gather_kernel, out_shape=jax.ShapeDtypeStruct((ny, nz, cor...  77.9 us
    pallas_call x1, Pallas kernels, local(): pl.pallas_call(sweep_kernel, out_shape=shape, in_specs=[smem] * 4 + [vmem...  21.9 us
    ppermute x3, starting transfers between devices, passed_along(): lax.ppermute(array, axis, [(i, (i + by) % count) for i in range(count)])  21.4 us
    all_gather x1, waiting for transfers between devices, local(): adjacency = lax.all_gather(a1_blocks, 'cols', axis=0, tiled=True)  7.27 us
    pallas_call x1, Pallas kernels, local(): pl.pallas_call(left_kernel, out_shape=shape, in_specs=[smem, smem, smem,...  7.13 us
    unnamed x1, blocking collectives  6.86 us
  transfers between devices with their start and end apart: 4, of which 1 were waited for; matrix products, arithmetic and copies ran while one was open for 4% of the time, Pallas kernels for 47%

profile of v2, /device:TPU:1, one launch (start us, length us, event | category | flops | bytes accessed | tf_op | source)
XLA Modules:
  0.0 166.0 jit_solution(13279026594745200049)
XLA Ops:
  6.5 0.0 all-gather.2.cloned.1.call-start
  6.5 0.7 all-gather.2.cloned.1.call-update
  7.3 1.3 slice.10
  8.6 8.7 %collective-permute-start.1 = (bf16[8,4,128,128]{3,2,1,0:T(8,128)(2,1)S(1)}, bf16[8,4,128,128]{3,2,1,0:T(8,128)(2,1)S(1)}, u32[]{:S(2)}, u32[]{:S(2)}) collective-permute-start(bf16[8,4,128,128]{3,2,1,0:T(8,128)(2,1)S(1)} %slice.10), channel_id=1, source_target_pairs={{0,508},{4,0},{8,4},{12,8},{16,12},{20,16},{24,20},{28,24},{32,28}... | collective-permute-start | bytes 3145736 | tf_op jit(solution)/shard_map/ppermute | solution.py:13
  17.3 0.0 copy-done.2
  17.3 0.1 slice.9
  17.4 0.1 copy.20
  17.5 7.9 %collective-permute-start = (s32[8,4]{1,0:T(8,128)S(1)}, s32[8,4]{1,0:T(8,128)S(1)}, u32[]{:S(2)}, u32[]{:S(2)}) collective-permute-start(s32[8,4]{1,0:T(8,128)S(1)} %copy.20), channel_id=1, source_target_pairs={{0,508},{4,0},{8,4},{12,8},{16,12},{20,16},{24,20},{28,24},{32,28}... | collective-permute-start | bytes 392 | tf_op jit(solution)/shard_map/ppermute | solution.py:13
  25.4 1.3 dynamic-slice
  27.4 0.0 copy-done.3
  27.4 0.2 dynamic-update-slice
  27.6 6.9 %all-reduce = s32[16]{0:T(128)S(1)} all-reduce(s32[16]{0:T(128)S(1)} %dynamic-update-slice), channel_id=1, replica_groups=mesh['rows'=128,'cols'=4] {'cols'}, use_global_device_ids=true, to_apply=%add | all-reduce | flops 16 | bytes 128
  34.5 0.6 broadcast_add_fusion.within
  35.1 0.0 collective-permute-done
  35.1 0.6 gather_fusion
  35.6 0.1 copy.16
  35.8 0.1 copy.18
  35.8 0.6 reshape.22.found
  36.5 0.1 copy.17
  36.6 0.6 reshape.18.chosen
  37.2 0.0 collective-permute-done.1.next_prior
  37.2 7.3 %all-gather.2.cloned.1.call-done.adjacency = bf16[16,2,128,128]{3,2,1,0:T(8,128)(2,1)} async-done(((bf16[4,2,128,128]{3,2,1,0:T(8,128)(2,1)}), bf16[16,2,128,128]{3,2,1,0:T(8,128)(2,1)}) %all-gather.2.cloned.1.call-update) | async-done | bytes 1048592 | tf_op jit(solution)/shard_map/all_gather | solution.py:294
  44.5 0.0 copy-done
  44.5 7.1 %shard_map.55.first = bf16[16,4,128,128]{3,2,1,0:T(8,128)(2,1)} custom-call(s32[16]{0:T(128)} %broadcast_add_fusion.within, s32[64]{0:T(128)} %reshape.18.chosen, s32[64]{0:T(128)} %reshape.22.found, bf16[16,4,128,128]{3,2,1,0:T(8,128)(2,1)} %prior.3, bf16[8,4,128,128]{3,2,1,0:T(8,128)(2,1)} %copy-done, ...), custom_call_target="tpu_custom_call" | custom-call | flops 536870912 | bytes 8388608 | tf_op jit(solution)/shard_map/pallas_call | solution.py:310
  51.6 1.3 slice.14
  52.9 4.7 %collective-permute-start.2 = (bf16[8,4,128,128]{3,2,1,0:T(8,128)(2,1)S(1)}, bf16[8,4,128,128]{3,2,1,0:T(8,128)(2,1)S(1)}, u32[]{:S(2)}, u32[]{:S(2)}) collective-permute-start(bf16[8,4,128,128]{3,2,1,0:T(8,128)(2,1)S(1)} %slice.14), channel_id=1, source_target_pairs={{0,508},{4,0},{8,4},{12,8},{16,12},{20,16},{24,20},{28,24},{32,28}... | collective-permute-start | bytes 3145736 | tf_op jit(solution)/shard_map/ppermute | solution.py:13
  57.7 0.1 copy.19
  57.7 0.6 reshape.19.place
  58.4 77.9 %shard_map.56 = bf16[4,16,2,512,128]{4,3,2,1,0:T(8,128)(2,1)} custom-call(bf16[512,128]{1,0:T(8,128)(2,1)} %bitcast.4), custom_call_target="tpu_custom_call" | custom-call | bytes 150000000 | tf_op jit(solution)/shard_map/pallas_call | solution.py:275
  136.3 0.0 collective-permute-done.2.next_first
  136.3 1.0 copy-done.1
  137.2 21.9 %shard_map.57 = bf16[16,4,128,128]{3,2,1,0:T(8,128)(2,1)} custom-call(s32[16]{0:T(128)} %broadcast_add_fusion.within, s32[64]{0:T(128)} %reshape.18.chosen, s32[64]{0:T(128)} %reshape.22.found, s32[64]{0:T(128)} %reshape.19.place, bf16[16,4,128,128]{3,2,1,0:T(8,128)(2,1)} %prior.3, bf16[8,4,128,128]{3,2,1,0:T(8,128)(2,1)} %copy-done, ...), custom_call_target="tpu_custom_call" | custom-call | flops 1610612736 | bytes 12582912 | tf_op jit(solution)/shard_map/pallas_call | solution.py:320
  (11 shorter events, 0.1 us)
Async XLA Ops:
  6.5 10.8 %copy-start.2 = (s32[16,4]{0,1:T(4,128)S(1)}, s32[16,4]{0,1:T(4,128)}, u32[]{:S(2)}) copy-start(s32[16,4]{0,1:T(4,128)} %param.6) | copy-start | bytes 772
  6.5 20.8 %copy-start.3 = (s32[4]{0:T(128)S(1)}, s32[4]{0:T(128)}, u32[]{:S(2)}) copy-start(s32[4]{0:T(128)} %param.7) | copy-start | bytes 52
  6.5 37.9 %all-gather.2.cloned.1.call-start = ((), (), s32[]{:S(2)}) async-start(), calls=%async_computation | async-start | bytes 1310720 | tf_op jit(solution)/shard_map/all_gather | solution.py:294
  8.6 28.6 %collective-permute-start.1 = (bf16[8,4,128,128]{3,2,1,0:T(8,128)(2,1)S(1)}, bf16[8,4,128,128]{3,2,1,0:T(8,128)(2,1)S(1)}, u32[]{:S(2)}, u32[]{:S(2)}) collective-permute-start(bf16[8,4,128,128]{3,2,1,0:T(8,128)(2,1)S(1)} %slice.10), channel_id=1, source_target_pairs={{0,508},{4,0},{8,4},{12,8},{16,12},{20,16},{24,20},{28,24},{32,28}... | collective-permute-start | bytes 3145736 | tf_op jit(solution)/shard_map/ppermute | solution.py:13
  17.5 17.6 %collective-permute-start = (s32[8,4]{1,0:T(8,128)S(1)}, s32[8,4]{1,0:T(8,128)S(1)}, u32[]{:S(2)}, u32[]{:S(2)}) collective-permute-start(s32[8,4]{1,0:T(8,128)S(1)} %copy.20), channel_id=1, source_target_pairs={{0,508},{4,0},{8,4},{12,8},{16,12},{20,16},{24,20},{28,24},{32,28}... | collective-permute-start | bytes 392 | tf_op jit(solution)/shard_map/ppermute | solution.py:13
  37.2 7.3 %copy-start = (bf16[8,4,128,128]{3,2,1,0:T(8,128)(2,1)}, bf16[8,4,128,128]{3,2,1,0:T(8,128)(2,1)S(1)}, u32[]{:S(2)}) copy-start(bf16[8,4,128,128]{3,2,1,0:T(8,128)(2,1)S(1)} %collective-permute-done.1.next_prior) | copy-start | bytes 3145732
  52.9 83.4 %collective-permute-start.2 = (bf16[8,4,128,128]{3,2,1,0:T(8,128)(2,1)S(1)}, bf16[8,4,128,128]{3,2,1,0:T(8,128)(2,1)S(1)}, u32[]{:S(2)}, u32[]{:S(2)}) collective-permute-start(bf16[8,4,128,128]{3,2,1,0:T(8,128)(2,1)S(1)} %slice.14), channel_id=1, source_target_pairs={{0,508},{4,0},{8,4},{12,8},{16,12},{20,16},{24,20},{28,24},{32,28}... | collective-permute-start | bytes 3145736 | tf_op jit(solution)/shard_map/ppermute | solution.py:13
  136.3 1.0 copy-start.1
Sparse Core Ops, SparseCore 0:
  9.4 34.9 all-gather.1

commit v3 on v2

v3 whole, which is shorter than its diff:
```python
import jax
import jax.numpy as jnp
from jax import lax
from jax.experimental import pallas as pl
from jax.experimental.pallas import tpu as pltpu
from jax.sharding import PartitionSpec as P

mixing = 0.75


def contract(a, b, dims):
    return lax.dot_general(a, b, (dims, ((), ())), preferred_element_type=jnp.float32)


MESH = pl.DeviceIdType.MESH
ny, nz, cores = 4, 16, 2


def propagate_kernel(
    meta, prior, a1, a2, out,
    whole, adjacency, next_prior, first, next_first, next_meta, col_meta,
    my_ids, next_ids, links, picks,
    own_sem, az_s, az_r, bz_s, bz_r, by_s, by_r, ay_s, ay_r, ah_s, ah_r, sib_s, sib_r,
    col_s, col_r, next_s, next_r, first_s, first_r, local_sem,
):
    rows, per, block = prior.shape[0], prior.shape[1], prior.shape[2]
    upper = rows // 2
    columns = adjacency.shape[0]
    row_share = rows // columns
    me, col = lax.axis_index("rows"), lax.axis_index("cols")
    core = lax.rem(me, cores)
    z = lax.rem(me // cores, nz)
    y = me // (cores * nz)
    height = a2.shape[0]
    cut = height * 3 // 4
    a_half, b_half = cut // 2, (height - cut) // 2
    a_all, b_all = pl.ds(0, cut), pl.ds(cut, height - cut)
    a_part = (pl.ds(0, a_half), pl.ds(a_half, a_half))
    b_part = (pl.ds(cut, b_half), pl.ds(cut + b_half, b_half))

    def zz(by):
        return lax.rem(z + by + nz, nz)

    def yy(by):
        return lax.rem(y + by + ny, ny)

    def device(y_at, z_at, core_at):
        return ((y_at * nz + z_at) * cores + core_at, col)

    z_to = (device(y, zz(1), core), device(y, zz(-1), core))
    y_to = (device(yy(1), z, core), device(yy(-1), z, core))
    sibling = device(y, z, 1 - core)
    sign = (-1, 1)
    slabs = ny * nz * cores
    before = (lax.rem(me + slabs - 1, slabs), col)
    after = (lax.rem(me + 1, slabs), col)
    col_to = tuple((me, lax.rem(col + by, columns)) for by in range(1, columns))

    barrier = pltpu.get_barrier_semaphore()
    for other in z_to + y_to + (sibling, before, after) + col_to:
        pl.semaphore_signal(barrier, inc=1, device_id=other, device_id_type=MESH)
    own = pltpu.make_async_copy(a2, whole.at[y, z, core], own_sem)
    own.start()
    own_a1 = pltpu.make_async_copy(a1, adjacency.at[col], local_sem.at[0])
    own_a1.start()
    own_links = pltpu.make_async_copy(meta, links.at[col], local_sem.at[1])
    own_links.start()
    own_ids = pltpu.make_async_copy(meta, my_ids, local_sem.at[2])
    own_ids.start()
    pl.semaphore_wait(barrier, 7 + columns - 1)

    def copy(src, dst, send_sem, recv_sem, to):
        return pltpu.make_async_remote_copy(
            src_ref=src, dst_ref=dst, send_sem=send_sem, recv_sem=recv_sem,
            device_id=to, device_id_type=MESH,
        )

    def az(d, s, part, mine=False):
        place = whole.at[y, zz(sign[d] * (s - 1)), core, part]
        return copy(a2.at[part] if mine else place, place, az_s.at[d, s], az_r.at[d, s], z_to[d])

    def az_in(d, s, part):
        place = whole.at[y, zz(sign[d] * s), core, part]
        copy(place, place, az_s.at[d, s], az_r.at[d, s], z_to[d]).wait_recv()

    def bz(d, s, part):
        place = whole.at[:, zz(sign[d] * (s - 1)), core, part]
        return copy(place, place, bz_s.at[d, s], bz_r.at[d, s], z_to[d])

    def bz_in(d, s, part):
        place = whole.at[:, zz(sign[d] * s), core, part]
        copy(place, place, bz_s.at[d, s], bz_r.at[d, s], z_to[d]).wait_recv()

    def by(d, h, y_at, part, mine=False):
        place = whole.at[y_at, z, core, part]
        return copy(a2.at[part] if mine else place, place, by_s.at[d, h], by_r.at[d, h], y_to[d])

    def ay(d, z_at, mine=False):
        place = whole.at[y, z_at, core, a_all]
        return copy(a2.at[a_all] if mine else place, place, ay_s.at[d, z_at], ay_r.at[d, z_at], y_to[d])

    def ay_in(d, z_at):
        place = whole.at[yy(sign[d]), z_at, core, a_all]
        copy(place, place, ay_s.at[d, z_at], ay_r.at[d, z_at], y_to[d]).wait_recv()

    def ah(d, y_at, z_at):
        place = whole.at[y_at, z_at, core, a_part[d]]
        return copy(place, place, ah_s.at[d, z_at], ah_r.at[d, z_at], y_to[d])

    def share(place):
        copy(place, place, sib_s, sib_r, sibling).start()

    def from_y(z_at):
        for d in range(2):
            ay_in(d, z_at)
            ah(d, yy(sign[d]), z_at).start()
            share(whole.at[yy(sign[d]), z_at, core, a_all])

    def from_y_far(z_at):
        for d in range(2):
            ah(d, yy(2), z_at).wait_recv()
        share(whole.at[yy(2), z_at, core, a_all])

    def a_step(s, last):
        for d in range(2):
            z_at = zz(sign[d] * s)
            az_in(d, s, a_all)
            az(d, s + 1, a_part[d] if last else a_all).start()
            for e in range(2):
                ay(e, z_at).start()
            share(whole.at[y, z_at, core, a_all])

    def b_step(s, last):
        for d in range(2):
            z_at = zz(sign[d] * s)
            bz_in(d, s, b_all)
            bz(d, s + 1, b_part[d] if last else b_all).start()
            share(whole.at[:, z_at, core, b_all])

    def col_a1(by, source):
        return copy(a1, adjacency.at[source], col_s.at[0, by], col_r.at[0, by], col_to[by - 1])

    def col_links(by, source):
        return copy(meta, col_meta.at[source], col_s.at[1, by], col_r.at[1, by], col_to[by - 1])

    def ids_along():
        return copy(meta, next_meta, next_s.at[0], next_r.at[0], before)

    def prior_along():
        return copy(prior.at[pl.ds(upper, upper)], next_prior, next_s.at[1], next_r.at[1], before)

    pair = upper // 4

    def first_along(part):
        here = first.at[pl.ds(upper + part * pair, pair)]
        there = next_first.at[pl.ds(part * pair, pair)]
        return copy(here, there, first_s.at[part], first_r.at[part], before)

    def left_row(i):
        owner, at = i // row_share, lax.rem(i, row_share)
        linked = lax.rem(links[owner, 1, at], upper)
        for k in range(per):
            n = i * per + k
            target = my_ids[0, n]
            chosen, found = jnp.int32(0), jnp.int32(0)
            for j in range(per):
                same = (next_ids[0, (linked + upper) * per + j] == target).astype(jnp.int32)
                chosen = chosen + same * j
                found = found + same
            picks[0, n] = linked
            chosen = lax.rem(chosen, per)
            picks[1, n] = chosen
            picks[2, n] = found
            picked = next_prior[linked, chosen]
            total = contract(adjacency[owner, at, 0], prior[i, k], ((1,), (0,)))
            cross = contract(adjacency[owner, at, 1], picked, ((1,), (0,)))
            total = total + cross * found.astype(jnp.float32)
            first[i, k] = total.astype(jnp.bfloat16)

    def sweep_row(i, carry):
        owner, at = i // row_share, lax.rem(i, row_share)
        for k in range(per):
            n = i * per + k
            name = my_ids[0, n]
            slab = lax.div(name, columns * targets)
            slab_y, slab_z = lax.div(slab, nz * cores), lax.rem(lax.div(slab, cores), nz)
            slab_core, low = lax.rem(slab, cores), lax.rem(name, targets) * 2
            target = jnp.concatenate(
                [
                    whole[slab_y, slab_z, slab_core, low],
                    whole[slab_y, slab_z, slab_core, low + 1],
                ],
                axis=0,
            )
            picked_prior = next_prior[picks[0, n], picks[1, n]]
            picked_first = next_first[picks[0, n], picks[1, n]]
            own_prior = prior[i, k]
            values = jnp.concatenate([first[i, k], picked_first], axis=0)
            base = jnp.concatenate([own_prior, picked_prior], axis=0).astype(jnp.float32)
            image = contract(values, target, ((1,), (1,)))
            swept = (mixing * image + (1.0 - mixing) * base).astype(jnp.bfloat16)
            carried = contract(swept, target, ((1,), (1,))).astype(jnp.bfloat16)
            total = contract(adjacency[owner, at, 0], carried[:block], ((1,), (0,)))
            cross = contract(adjacency[owner, at, 1], carried[block:], ((1,), (0,)))
            total = total + cross * picks[2, n].astype(jnp.float32)
            out[i, k] = (mixing * total + (1.0 - mixing) * own_prior.astype(jnp.float32)).astype(
                jnp.bfloat16
            )
        return carry

    def left_rows(s):
        for i in range(pair):
            left_row(upper + (s - 3) * pair + i)
        for i in range(pair):
            left_row((s - 3) * pair + i)

    targets = whole.shape[3] // 2
    ids_along().start()
    for by_col in range(1, columns):
        col_links(by_col, col).start()
        col_a1(by_col, col).start()
    for d in range(2):
        az(d, 1, a_all, True).start()
        by(d, 0, y, b_all, True).start()
    for d in range(2):
        ay(d, z, True).start()
    prior_along().start()
    for d in range(2):
        by(d, 0, yy(sign[d]), b_all).wait_recv()
        by(d, 1, yy(sign[d]), b_part[d]).start()
    own.wait()
    share(whole.at[y, z, core, a_all])
    a_step(1, False)
    for d in range(2):
        by(d, 1, yy(2), b_part[d]).wait_recv()
    for d in range(2):
        bz(d, 1, b_all).start()
    share(whole.at[:, z, core, b_all])
    from_y(z)
    a_step(2, False)
    from_y_far(z)
    for d in range(2):
        from_y(zz(sign[d]))
    b_step(1, False)

    own_ids.wait()
    own_links.wait()
    own_a1.wait()
    ids_along().wait_recv()
    to_smem = pltpu.make_async_copy(next_meta, next_ids, local_sem.at[2])
    to_smem.start()
    for by_col in range(1, columns):
        source = lax.rem(col + columns - by_col, columns)
        col_links(by_col, source).wait_recv()
        moved = pltpu.make_async_copy(col_meta.at[source], links.at[source], local_sem.at[1])
        moved.start()
        moved.wait()
        col_a1(by_col, source).wait_recv()
    to_smem.wait()
    prior_along().wait_recv()

    def steady(s, carry):
        a_step(s, False)
        if not isinstance(s, int):
            first_along(s - 4).start()
        for d in range(2):
            from_y_far(zz(sign[d] * (s - 2)))
        for d in range(2):
            from_y(zz(sign[d] * (s - 1)))
        b_step(s - 1, False)
        left_rows(s)
        return carry

    far = nz // 2
    steady(3, 0)
    lax.fori_loop(4, far - 1, steady, 0)
    a_step(far - 1, True)
    first_along(3).start()
    for d in range(2):
        from_y_far(zz(sign[d] * (far - 3)))
    for d in range(2):
        from_y(zz(sign[d] * (far - 2)))
    b_step(far - 2, False)
    for d in range(2):
        az_in(d, far, a_part[d])
    for e in range(2):
        ay(e, zz(far)).start()
    share(whole.at[y, zz(far), core, a_all])
    for d in range(2):
        from_y_far(zz(sign[d] * (far - 2)))
    for d in range(2):
        from_y(zz(sign[d] * (far - 1)))
    b_step(far - 1, True)
    from_y(zz(far))
    for d in range(2):
        from_y_far(zz(sign[d] * (far - 1)))
    for d in range(2):
        bz_in(d, far, b_part[d])
    share(whole.at[:, zz(far), core, b_all])
    from_y_far(zz(far))

    for d in range(2):
        by(d, 0, y, b_all).wait_send()
        by(d, 1, y, b_part[d]).wait_send()
        az(d, far, a_part[d]).wait_send()
        bz(d, far, b_part[d]).wait_send()

    def sent_z(s, carry):
        for d in range(2):
            az(d, s, a_all).wait_send()
            bz(d, s, b_all).wait_send()
        return carry

    lax.fori_loop(1, far, sent_z, 0)

    def sent_y(z_at, carry):
        for d in range(2):
            ay(d, z_at).wait_send()
            ah(d, y, z_at).wait_send()
        return carry

    lax.fori_loop(0, nz, sent_y, 0)
    mine, theirs = whole.at[:, :, core], whole.at[:, :, 1 - core]
    copy(mine, mine, sib_s, sib_r, sibling).wait_send()
    copy(theirs, theirs, sib_s, sib_r, sibling).wait_recv()
    ids_along().wait_send()
    prior_along().wait_send()
    for by_col in range(1, columns):
        col_links(by_col, col).wait_send()
        col_a1(by_col, col).wait_send()
    for part in range(4):
        first_along(part).wait_send()
        first_along(part).wait_recv()
    lax.fori_loop(0, rows, sweep_row, 0)


def local(prior, candidates, cross_link, a1_blocks, a2_blocks):
    rows, per, block = prior.shape[0], prior.shape[1], prior.shape[2]
    columns = lax.axis_size("cols")
    targets_here = a2_blocks.shape[0]
    upper = rows // 2
    pieces = a2_blocks.reshape(2 * targets_here, block // 2, block)
    far = nz // 2
    lanes = 128
    ids = jnp.pad(candidates.reshape(1, -1), ((0, 0), (0, lanes - candidates.size)))
    names = jnp.pad(cross_link.reshape(1, -1), ((0, 6), (0, lanes - cross_link.size)))
    meta = jnp.concatenate([ids, names], axis=0)
    tile = meta.shape
    dma = pltpu.SemaphoreType.DMA
    zs, ys = dma((2, far + 1)), dma((2, nz))
    vmem = pl.BlockSpec(memory_space=pltpu.VMEM)
    half = (upper,) + prior.shape[1:]
    return pl.pallas_call(
        propagate_kernel,
        out_shape=jax.ShapeDtypeStruct(prior.shape, prior.dtype),
        in_specs=[vmem] * 4,
        out_specs=vmem,
        scratch_shapes=[
            pltpu.VMEM((ny, nz, cores) + pieces.shape, jnp.bfloat16),
            pltpu.VMEM((columns,) + a1_blocks.shape, jnp.bfloat16),
            pltpu.VMEM(half, jnp.bfloat16),
            pltpu.VMEM(prior.shape, jnp.bfloat16),
            pltpu.VMEM(half, jnp.bfloat16),
            pltpu.VMEM(tile, jnp.int32),
            pltpu.VMEM((columns,) + tile, jnp.int32),
            pltpu.SMEM(tile, jnp.int32),
            pltpu.SMEM(tile, jnp.int32),
            pltpu.SMEM((columns,) + tile, jnp.int32),
            pltpu.SMEM(tile, jnp.int32),
        ]
        + [dma(())]
        + [zs] * 4
        + [dma((2, 2))] * 2
        + [ys] * 4
        + [dma(())] * 2
        + [dma((2, columns))] * 2
        + [dma((2,))] * 2
        + [dma((4,))] * 2
        + [dma((3,))],
        compiler_params=pltpu.CompilerParams(collective_id=0, has_side_effects=True),
    )(meta, prior, a1_blocks, pieces)


def solution(mesh):
    placed = (
        P("rows", "cols", None, None),
        P("rows", "cols"),
        P(("rows", "cols")),
        P(("rows", "cols"), None, None, None),
        P(("rows", "cols"), None, None),
    )
    return jax.shard_map(
        local, mesh=mesh, in_specs=placed, out_specs=P("rows", "cols", None, None), check_vma=False
    )
```

time: 166 us -> 123 us (0.74)
  starting transfers between devices: 21.4 us -> 0 us
  between operations: 14.2 us -> 0.01 us
  Pallas kernels: 107 us -> 117 us
  waiting for transfers between devices: 7.99 us -> 0 us
  blocking collectives: 6.86 us -> 0 us
  local copies, waits for them, and re-layouts: 8.02 us -> 4 us
    ppermute x3 -> x0, starting transfers between devices: 21.4 us -> none  [passed_along(): lax.ppermute(array, axis, [(i, (i + by) % count) for i in range(count)])]
    pallas_call x3 -> x1, Pallas kernels: 107 us -> 117 us  [local(): pl.pallas_call(propagate_kernel, out_shape=jax.ShapeDtypeStruct(prior.sha...]
    all_gather x1 -> x0, waiting for transfers between devices: 7.27 us -> none  [local(): adjacency = lax.all_gather(a1_blocks, 'cols', axis=0, tiled=True)]
    unnamed x1 -> x0, blocking collectives: 6.86 us -> none
    slice x3 -> x0, local copies, waits for them, and re-layouts: 2.66 us -> none  [the longest x1 1.3 us: local(): next_prior = passed_along(prior[upper_half:], 'rows', -1)]
    unnamed x12 -> x2, local copies, waits for them, and re-layouts: 2.58 us -> 3.92 us
  transfers between devices with their start and end apart: 4 -> 0, of which waited for: 1 -> 0; matrix products, arithmetic and copies ran while one was open for 4% -> 0% of each run, Pallas kernels for 47% -> 0%
where the time goes in v3:
time: 123 us; the launch traced here: 122 us
  Pallas kernels  117 us (95%)
  local copies, waits for them, and re-layouts  4 us (3%)
  other arithmetic  1.26 us (1%)
    pallas_call x1, Pallas kernels, local(): pl.pallas_call(propagate_kernel, out_shape=jax.ShapeDtypeStruct(prior.sha...  117 us
    unnamed x2, local copies, waits for them, and re-layouts  3.92 us

profile of v3, /device:TPU:1, one launch (start us, length us, event | category | flops | bytes accessed | tf_op | source)
XLA Modules:
  0.0 122.3 jit_solution(12428770377115862942)
XLA Ops:
  0.0 0.8 copy.7
  0.8 0.1 reshape.9
  0.8 1.3 %pad_add_fusion.meta = s32[8,128]{1,0:T(8,128)} fusion(s32[1,4]{1,0:T(1,128)} %bitcast.3, s32[1,64]{1,0:T(1,128)S(1)} %reshape.9), kind=kLoop, calls=%fused_computation | loop fusion | flops 1024 | bytes 4368 | tf_op jit(solution)/shard_map/concatenate | solution.py:347
  2.1 117.1 %shard_map.55 = bf16[16,4,128,128]{3,2,1,0:T(8,128)(2,1)} custom-call(s32[8,128]{1,0:T(8,128)} %pad_add_fusion.meta, bf16[16,4,128,128]{3,2,1,0:T(8,128)(2,1)} %prior.1, bf16[4,2,128,128]{3,2,1,0:T(8,128)(2,1)} %a1.1, bf16[8,64,128]{2,1,0:T(8,128)(2,1)} %bitcast.2), custom_call_target="tpu_custom_call" | custom-call | tf_op jit(solution)/shard_map/pallas_call | solution.py:353
  119.2 3.2 %copy.9 = bf16[16,4,128,128]{3,2,1,0:T(8,128)(2,1)} copy(bf16[16,4,128,128]{3,2,1,0:T(8,128)(2,1)} %shard_map.55) | data formatting | bytes 4194304

commit v4 on v3

--- a/solution.py
+++ b/solution.py
@@ -14,6 +14,7 @@
 
 MESH = pl.DeviceIdType.MESH
 ny, nz, cores = 4, 16, 2
+hops = (9, 6)
 
 
 def propagate_kernel(
@@ -121,20 +122,28 @@
             ah(d, yy(2), z_at).wait_recv()
         share(whole.at[yy(2), z_at, core, a_all])
 
-    def a_step(s, last):
-        for d in range(2):
+    def going(s):
+        return [d for d in range(2) if s <= hops[d]]
+
+    def sources(s):
+        return [zz(sign[d] * s) for d in going(s)] if s else [z]
+
+    def a_step(s):
+        for d in going(s):
             z_at = zz(sign[d] * s)
             az_in(d, s, a_all)
-            az(d, s + 1, a_part[d] if last else a_all).start()
+            if s < hops[d]:
+                az(d, s + 1, a_all).start()
             for e in range(2):
                 ay(e, z_at).start()
             share(whole.at[y, z_at, core, a_all])
 
-    def b_step(s, last):
-        for d in range(2):
+    def b_step(s):
+        for d in going(s):
             z_at = zz(sign[d] * s)
             bz_in(d, s, b_all)
-            bz(d, s + 1, b_part[d] if last else b_all).start()
+            if s < hops[d]:
+                bz(d, s + 1, b_all).start()
             share(whole.at[:, z_at, core, b_all])
 
     def col_a1(by, source):
@@ -177,42 +186,60 @@
             total = total + cross * found.astype(jnp.float32)
             first[i, k] = total.astype(jnp.bfloat16)
 
+    def target_of(n):
+        name = my_ids[0, n]
+        slab = lax.div(name, columns * targets)
+        slab_y, slab_z = lax.div(slab, nz * cores), lax.rem(lax.div(slab, cores), nz)
+        slab_core, low = lax.rem(slab, cores), lax.rem(name, targets) * 2
+        upper_part = whole[slab_y, slab_z, slab_core, low]
+        return jnp.concatenate([upper_part, whole[slab_y, slab_z, slab_core, low + 1]], axis=0)
+
+    def square(a, b, c, d):
+        top, bottom = jnp.concatenate([a, b], axis=1), jnp.concatenate([c, d], axis=1)
+        return jnp.concatenate([top, bottom], axis=0)
+
     def sweep_row(i, carry):
         owner, at = i // row_share, lax.rem(i, row_share)
-        for k in range(per):
-            n = i * per + k
-            name = my_ids[0, n]
-            slab = lax.div(name, columns * targets)
-            slab_y, slab_z = lax.div(slab, nz * cores), lax.rem(lax.div(slab, cores), nz)
-            slab_core, low = lax.rem(slab, cores), lax.rem(name, targets) * 2
-            target = jnp.concatenate(
-                [
-                    whole[slab_y, slab_z, slab_core, low],
-                    whole[slab_y, slab_z, slab_core, low + 1],
-                ],
-                axis=0,
+        weights = jnp.concatenate([adjacency[owner, at, 0], adjacency[owner, at, 1]], axis=1)
+        for k in range(0, per, 2):
+            n, m = i * per + k, i * per + k + 1
+            one, two = target_of(n), target_of(m)
+            zero = jnp.zeros_like(one)
+            both = square(one, zero, zero, two)
+            values = square(
+                first[i, k],
+                first[i, k + 1],
+                next_first[picks[0, n], picks[1, n]],
+                next_first[picks[0, m], picks[1, m]],
             )
-            picked_prior = next_prior[picks[0, n], picks[1, n]]
-            picked_first = next_first[picks[0, n], picks[1, n]]
-            own_prior = prior[i, k]
-            values = jnp.concatenate([first[i, k], picked_first], axis=0)
-            base = jnp.concatenate([own_prior, picked_prior], axis=0).astype(jnp.float32)
-            image = contract(values, target, ((1,), (1,)))
+            base = square(
+                prior[i, k],
+                prior[i, k + 1],
+                next_prior[picks[0, n], picks[1, n]],
+                next_prior[picks[0, m], picks[1, m]],
+            ).astype(jnp.float32)
+            image = contract(values, both, ((1,), (1,)))
             swept = (mixing * image + (1.0 - mixing) * base).astype(jnp.bfloat16)
-            carried = contract(swept, target, ((1,), (1,))).astype(jnp.bfloat16)
-            total = contract(adjacency[owner, at, 0], carried[:block], ((1,), (0,)))
-            cross = contract(adjacency[owner, at, 1], carried[block:], ((1,), (0,)))
-            total = total + cross * picks[2, n].astype(jnp.float32)
-            out[i, k] = (mixing * total + (1.0 - mixing) * own_prior.astype(jnp.float32)).astype(
-                jnp.bfloat16
-            )
+            carried = contract(swept, both, ((1,), (1,)))
+            stacked = square(
+                carried[:block, :block],
+                carried[:block, block:],
+                carried[block:, :block] * picks[2, n].astype(jnp.float32),
+                carried[block:, block:] * picks[2, m].astype(jnp.float32),
+            ).astype(jnp.bfloat16)
+            total = contract(weights, stacked, ((1,), (0,)))
+            mixed = (mixing * total + (1.0 - mixing) * base[:block]).astype(jnp.bfloat16)
+            out[i, k] = mixed[:, :block]
+            out[i, k + 1] = mixed[:, block:]
         return carry
 
     def left_rows(s):
-        for i in range(pair):
+        def one(i, carry):
             left_row(upper + (s - 3) * pair + i)
-        for i in range(pair):
             left_row((s - 3) * pair + i)
+            return carry
+
+        lax.fori_loop(0, pair, one, 0)
 
     targets = whole.shape[3] // 2
     ids_along().start()
@@ -230,19 +257,18 @@
         by(d, 1, yy(sign[d]), b_part[d]).start()
     own.wait()
     share(whole.at[y, z, core, a_all])
-    a_step(1, False)
+    a_step(1)
     for d in range(2):
         by(d, 1, yy(2), b_part[d]).wait_recv()
     for d in range(2):
         bz(d, 1, b_all).start()
     share(whole.at[:, z, core, b_all])
     from_y(z)
-    a_step(2, False)
+    a_step(2)
+    b_step(1)
     from_y_far(z)
-    for d in range(2):
-        from_y(zz(sign[d]))
-    b_step(1, False)
-
+    for z_at in sources(1):
+        from_y(z_at)
     own_ids.wait()
     own_links.wait()
     own_a1.wait()
@@ -259,59 +285,30 @@
     to_smem.wait()
     prior_along().wait_recv()
 
-    def steady(s, carry):
-        a_step(s, False)
-        if not isinstance(s, int):
+    longest = max(hops)
+    for s in range(3, longest + 2):
+        a_step(s)
+        b_step(s - 1)
+        if 4 <= s < 8:
             first_along(s - 4).start()
-        for d in range(2):
-            from_y_far(zz(sign[d] * (s - 2)))
-        for d in range(2):
-            from_y(zz(sign[d] * (s - 1)))
-        b_step(s - 1, False)
-        left_rows(s)
-        return carry
-
-    far = nz // 2
-    steady(3, 0)
-    lax.fori_loop(4, far - 1, steady, 0)
-    a_step(far - 1, True)
-    first_along(3).start()
-    for d in range(2):
-        from_y_far(zz(sign[d] * (far - 3)))
-    for d in range(2):
-        from_y(zz(sign[d] * (far - 2)))
-    b_step(far - 2, False)
-    for d in range(2):
-        az_in(d, far, a_part[d])
-    for e in range(2):
-        ay(e, zz(far)).start()
-    share(whole.at[y, zz(far), core, a_all])
-    for d in range(2):
-        from_y_far(zz(sign[d] * (far - 2)))
-    for d in range(2):
-        from_y(zz(sign[d] * (far - 1)))
-    b_step(far - 1, True)
-    from_y(zz(far))
-    for d in range(2):
-        from_y_far(zz(sign[d] * (far - 1)))
-    for d in range(2):
-        bz_in(d, far, b_part[d])
-    share(whole.at[:, zz(far), core, b_all])
-    from_y_far(zz(far))
-
+        for z_at in sources(s - 2):
+            from_y_far(z_at)
+        for z_at in sources(s - 1):
+            from_y(z_at)
+        if s < 7:
+            left_rows(s)
+    for z_at in sources(longest):
+        from_y_far(z_at)
     for d in range(2):
         by(d, 0, y, b_all).wait_send()
         by(d, 1, y, b_part[d]).wait_send()
-        az(d, far, a_part[d]).wait_send()
-        bz(d, far, b_part[d]).wait_send()
-
-    def sent_z(s, carry):
-        for d in range(2):
+
+        def sent_z(s, carry, d=d):
             az(d, s, a_all).wait_send()
             bz(d, s, b_all).wait_send()
-        return carry
-
-    lax.fori_loop(1, far, sent_z, 0)
+            return carry
+
+        lax.fori_loop(1, hops[d] + 1, sent_z, 0)
 
     def sent_y(z_at, carry):
         for d in range(2):
@@ -340,14 +337,13 @@
     targets_here = a2_blocks.shape[0]
     upper = rows // 2
     pieces = a2_blocks.reshape(2 * targets_here, block // 2, block)
-    far = nz // 2
     lanes = 128
     ids = jnp.pad(candidates.reshape(1, -1), ((0, 0), (0, lanes - candidates.size)))
     names = jnp.pad(cross_link.reshape(1, -1), ((0, 6), (0, lanes - cross_link.size)))
     meta = jnp.concatenate([ids, names], axis=0)
     tile = meta.shape
     dma = pltpu.SemaphoreType.DMA
-    zs, ys = dma((2, far + 1)), dma((2, nz))
+    zs, ys = dma((2, max(hops) + 1)), dma((2, nz))
     vmem = pl.BlockSpec(memory_space=pltpu.VMEM)
     half = (upper,) + prior.shape[1:]
     return pl.pallas_call(

time: 123 us -> 119 us (0.967)
  Pallas kernels: 117 us -> 113 us
    pallas_call x1, Pallas kernels: 117 us -> 113 us  [local(): pl.pallas_call(propagate_kernel, out_shape=jax.ShapeDtypeStruct(prior.sha...]
where the time goes in v4:
time: 119 us
  Pallas kernels  113 us (95%)
  local copies, waits for them, and re-layouts  4 us (3%)
  other arithmetic  1.26 us (1%)
    pallas_call x1, Pallas kernels, local(): pl.pallas_call(propagate_kernel, out_shape=jax.ShapeDtypeStruct(prior.sha...  113 us
    unnamed x2, local copies, waits for them, and re-layouts  3.92 us

profile of v4, /device:TPU:1, one launch (start us, length us, event | category | flops | bytes accessed | tf_op | source)
XLA Modules:
  0.0 118.7 jit_solution(16306555844249128542)
XLA Ops:
  0.0 0.8 copy.7
  0.8 0.1 reshape.9
  0.8 1.3 %pad_add_fusion.meta = s32[8,128]{1,0:T(8,128)} fusion(s32[1,4]{1,0:T(1,128)} %bitcast.3, s32[1,64]{1,0:T(1,128)S(1)} %reshape.9), kind=kLoop, calls=%fused_computation | loop fusion | flops 1024 | bytes 4368 | tf_op jit(solution)/shard_map/concatenate | solution.py:343
  2.1 113.4 %shard_map.55 = bf16[16,4,128,128]{3,2,1,0:T(8,128)(2,1)} custom-call(s32[8,128]{1,0:T(8,128)} %pad_add_fusion.meta, bf16[16,4,128,128]{3,2,1,0:T(8,128)(2,1)} %prior.1, bf16[4,2,128,128]{3,2,1,0:T(8,128)(2,1)} %a1.1, bf16[8,64,128]{2,1,0:T(8,128)(2,1)} %bitcast.2), custom_call_target="tpu_custom_call" | custom-call | tf_op jit(solution)/shard_map/pallas_call | solution.py:349
  115.5 3.2 %copy.9 = bf16[16,4,128,128]{3,2,1,0:T(8,128)(2,1)} copy(bf16[16,4,128,128]{3,2,1,0:T(8,128)(2,1)} %shard_map.55) | data formatting | bytes 4194304

commit v5 on v4

--- a/solution.py
+++ b/solution.py
@@ -235,8 +235,8 @@
 
     def left_rows(s):
         def one(i, carry):
-            left_row(upper + (s - 3) * pair + i)
-            left_row((s - 3) * pair + i)
+            left_row(upper + s * pair + i)
+            left_row(s * pair + i)
             return carry
 
         lax.fori_loop(0, pair, one, 0)
@@ -263,42 +263,38 @@
     for d in range(2):
         bz(d, 1, b_all).start()
     share(whole.at[:, z, core, b_all])
-    from_y(z)
-    a_step(2)
-    b_step(1)
-    from_y_far(z)
-    for z_at in sources(1):
-        from_y(z_at)
-    own_ids.wait()
-    own_links.wait()
-    own_a1.wait()
-    ids_along().wait_recv()
-    to_smem = pltpu.make_async_copy(next_meta, next_ids, local_sem.at[2])
-    to_smem.start()
-    for by_col in range(1, columns):
-        source = lax.rem(col + columns - by_col, columns)
-        col_links(by_col, source).wait_recv()
-        moved = pltpu.make_async_copy(col_meta.at[source], links.at[source], local_sem.at[1])
-        moved.start()
-        moved.wait()
-        col_a1(by_col, source).wait_recv()
-    to_smem.wait()
-    prior_along().wait_recv()
+    def ready():
+        own_ids.wait()
+        own_links.wait()
+        own_a1.wait()
+        ids_along().wait_recv()
+        to_smem = pltpu.make_async_copy(next_meta, next_ids, local_sem.at[2])
+        to_smem.start()
+        for by_col in range(1, columns):
+            source = lax.rem(col + columns - by_col, columns)
+            col_links(by_col, source).wait_recv()
+            moved = pltpu.make_async_copy(col_meta.at[source], links.at[source], local_sem.at[1])
+            moved.start()
+            moved.wait()
+            col_a1(by_col, source).wait_recv()
+        to_smem.wait()
+        prior_along().wait_recv()
 
     longest = max(hops)
-    for s in range(3, longest + 2):
+    for s in range(2, longest + 5):
         a_step(s)
         b_step(s - 1)
-        if 4 <= s < 8:
-            first_along(s - 4).start()
+        if 6 <= s < 10:
+            first_along(s - 6).start()
         for z_at in sources(s - 2):
-            from_y_far(z_at)
-        for z_at in sources(s - 1):
             from_y(z_at)
-        if s < 7:
-            left_rows(s)
-    for z_at in sources(longest):
-        from_y_far(z_at)
+        if s >= 4:
+            for z_at in sources(s - 4):
+                from_y_far(z_at)
+        if s == 5:
+            ready()
+        if 5 <= s < 9:
+            left_rows(s - 5)
     for d in range(2):
         by(d, 0, y, b_all).wait_send()
         by(d, 1, y, b_part[d]).wait_send()

time: 119 us -> 117 us (0.983)
  Pallas kernels: 113 us -> 111 us
    pallas_call x1, Pallas kernels: 113 us -> 111 us  [local(): pl.pallas_call(propagate_kernel, out_shape=jax.ShapeDtypeStruct(prior.sha...]
where the time goes in v5:
time: 117 us; the launch traced here: 116 us
  Pallas kernels  111 us (95%)
  local copies, waits for them, and re-layouts  4 us (3%)
  other arithmetic  1.26 us (1%)
    pallas_call x1, Pallas kernels, local(): pl.pallas_call(propagate_kernel, out_shape=jax.ShapeDtypeStruct(prior.sha...  111 us
    unnamed x2, local copies, waits for them, and re-layouts  3.92 us

profile of v5, /device:TPU:1, one launch (start us, length us, event | category | flops | bytes accessed | tf_op | source)
XLA Modules:
  0.0 116.3 jit_solution(9021066642443490286)
XLA Ops:
  0.0 0.8 copy.7
  0.8 0.1 reshape.9
  0.8 1.3 %pad_add_fusion.meta = s32[8,128]{1,0:T(8,128)} fusion(s32[1,4]{1,0:T(1,128)} %bitcast.3, s32[1,64]{1,0:T(1,128)S(1)} %reshape.9), kind=kLoop, calls=%fused_computation | loop fusion | flops 1024 | bytes 4368 | tf_op jit(solution)/shard_map/concatenate | solution.py:339
  2.1 111.0 %shard_map.55 = bf16[16,4,128,128]{3,2,1,0:T(8,128)(2,1)} custom-call(s32[8,128]{1,0:T(8,128)} %pad_add_fusion.meta, bf16[16,4,128,128]{3,2,1,0:T(8,128)(2,1)} %prior.1, bf16[4,2,128,128]{3,2,1,0:T(8,128)(2,1)} %a1.1, bf16[8,64,128]{2,1,0:T(8,128)(2,1)} %bitcast.2), custom_call_target="tpu_custom_call" | custom-call | tf_op jit(solution)/shard_map/pallas_call | solution.py:345
  113.1 3.2 %copy.9 = bf16[16,4,128,128]{3,2,1,0:T(8,128)(2,1)} copy(bf16[16,4,128,128]{3,2,1,0:T(8,128)(2,1)} %shard_map.55) | data formatting | bytes 4194304

commit v6 on v5

--- a/solution.py
+++ b/solution.py
@@ -155,10 +155,12 @@
     def ids_along():
         return copy(meta, next_meta, next_s.at[0], next_r.at[0], before)
 
-    def prior_along():
-        return copy(prior.at[pl.ds(upper, upper)], next_prior, next_s.at[1], next_r.at[1], before)
-
     pair = upper // 4
+
+    def prior_along(part):
+        here = prior.at[pl.ds(upper + part * pair, pair)]
+        there = next_prior.at[pl.ds(part * pair, pair)]
+        return copy(here, there, next_s.at[1 + part], next_r.at[1 + part], before)
 
     def first_along(part):
         here = first.at[pl.ds(upper + part * pair, pair)]
@@ -251,7 +253,6 @@
         by(d, 0, y, b_all, True).start()
     for d in range(2):
         ay(d, z, True).start()
-    prior_along().start()
     for d in range(2):
         by(d, 0, yy(sign[d]), b_all).wait_recv()
         by(d, 1, yy(sign[d]), b_part[d]).start()
@@ -278,23 +279,26 @@
             moved.wait()
             col_a1(by_col, source).wait_recv()
         to_smem.wait()
-        prior_along().wait_recv()
+        for part in range(4):
+            prior_along(part).wait_recv()
 
     longest = max(hops)
     for s in range(2, longest + 5):
         a_step(s)
         b_step(s - 1)
-        if 6 <= s < 10:
-            first_along(s - 6).start()
+        if 3 <= s < 7:
+            prior_along(s - 3).start()
+        if 9 <= s < 13:
+            first_along(s - 9).start()
         for z_at in sources(s - 2):
             from_y(z_at)
         if s >= 4:
             for z_at in sources(s - 4):
                 from_y_far(z_at)
-        if s == 5:
+        if s == 8:
             ready()
-        if 5 <= s < 9:
-            left_rows(s - 5)
+        if 8 <= s < 12:
+            left_rows(s - 8)
     for d in range(2):
         by(d, 0, y, b_all).wait_send()
         by(d, 1, y, b_part[d]).wait_send()
@@ -317,7 +321,8 @@
     copy(mine, mine, sib_s, sib_r, sibling).wait_send()
     copy(theirs, theirs, sib_s, sib_r, sibling).wait_recv()
     ids_along().wait_send()
-    prior_along().wait_send()
+    for part in range(4):
+        prior_along(part).wait_send()
     for by_col in range(1, columns):
         col_links(by_col, col).wait_send()
         col_a1(by_col, col).wait_send()
@@ -366,7 +371,7 @@
         + [ys] * 4
         + [dma(())] * 2
         + [dma((2, columns))] * 2
-        + [dma((2,))] * 2
+        + [dma((5,))] * 2
         + [dma((4,))] * 2
         + [dma((3,))],
         compiler_params=pltpu.CompilerParams(collective_id=0, has_side_effects=True),

time: 117 us -> 109 us (0.932)
  the two profiles are of different devices: /device:TPU:1 before, /device:TPU:449 now
where the time goes in v6:
time: 109 us
  Pallas kernels  104 us (95%)
  local copies, waits for them, and re-layouts  4 us (4%)
  other arithmetic  1.26 us (1%)
    pallas_call x1, Pallas kernels, local(): pl.pallas_call(propagate_kernel, out_shape=jax.ShapeDtypeStruct(prior.sha...  104 us
    unnamed x2, local copies, waits for them, and re-layouts  3.92 us

profile of v6, /device:TPU:449, one launch (start us, length us, event | category | flops | bytes accessed | tf_op | source)
XLA Modules:
  0.0 108.8 jit_solution(6998523184200976174)
XLA Ops:
  0.0 0.8 copy.7
  0.8 0.1 reshape.9
  0.8 1.3 %pad_add_fusion.meta = s32[8,128]{1,0:T(8,128)} fusion(s32[1,4]{1,0:T(1,128)} %bitcast.3, s32[1,64]{1,0:T(1,128)S(1)} %reshape.9), kind=kLoop, calls=%fused_computation | loop fusion | flops 1024 | bytes 4368 | tf_op jit(solution)/shard_map/concatenate | solution.py:344
  2.1 103.6 %shard_map.55 = bf16[16,4,128,128]{3,2,1,0:T(8,128)(2,1)} custom-call(s32[8,128]{1,0:T(8,128)} %pad_add_fusion.meta, bf16[16,4,128,128]{3,2,1,0:T(8,128)(2,1)} %prior.1, bf16[4,2,128,128]{3,2,1,0:T(8,128)(2,1)} %a1.1, bf16[8,64,128]{2,1,0:T(8,128)(2,1)} %bitcast.2), custom_call_target="tpu_custom_call" | custom-call | tf_op jit(solution)/shard_map/pallas_call | solution.py:350
  105.7 3.2 %copy.9 = bf16[16,4,128,128]{3,2,1,0:T(8,128)(2,1)} copy(bf16[16,4,128,128]{3,2,1,0:T(8,128)(2,1)} %shard_map.55) | data formatting | bytes 4194304
